TPU v7x, 32 devices: a whole 2x2x4 slice. The times are simulated.
32 devices in a mesh: sect: 2 (over x), slab: 8 (over z, y), energy: 2 (over core).
Axes of the slice: x: 2, y: 2, z: 4, core: 2. Of those that a mesh axis runs over, the one named last changes fastest.
Arguments:
- source: bfloat16 [4, 512, 128], P(('energy', 'sect'), 'slab'), parts along dimension 0, may hold values from -6 to 6
- forward_mult: bfloat16 [4, 2, 512, 512], P(('energy', 'sect'), None, 'slab'), parts along dimension 0, may hold values from -0.1875 to 0.1875
- schur_inverse: bfloat16 [4, 2, 512, 512], P(('energy', 'sect'), None, 'slab'), parts along dimension 0, may hold values from -0.09375 to 0.09375
- upper_mult: bfloat16 [4, 2, 512, 512], P(('energy', 'sect'), None, 'slab'), parts along dimension 0, may hold values from -0.125 to 0.125
Outputs:
- wave: bfloat16 [4, 512, 128], P(('energy', 'sect'), 'slab'), parts along dimension 0
There are 2 independent parts, one for each index of `energy`. A program takes and returns all parts, laid end to end along the dimension named above; each array names one. Nothing has to cross between parts.
All inputs are finite; a program needn't handle non-finite values.
Results may differ from a plain program's by a relative error of at most 0.012.
Values may be sent and summed in bfloat16 or wider, within the bound.
No kernel may reach another device: no remote copies, remote signals or barrier semaphores. Data moves between devices by JAX's collectives and lax.ppermute only.
A program may use at most 64 MiB of HBM per device.

v0:
```python
import jax
import jax.numpy as jnp
from jax import lax
from jax.sharding import PartitionSpec as P


def from_behind(block, axis, distance):
    devices = range(lax.axis_size(axis))
    route = [(i - distance, i) for i in devices if i - distance in devices]
    return lax.ppermute(block, axis, route)


def complex_apply(matrix, vector):
    half_cols = vector.shape[1] // 2
    real_part = jnp.dot(matrix[0], vector, preferred_element_type=jnp.float32)
    imag_part = jnp.dot(matrix[1], vector, preferred_element_type=jnp.float32)
    return jnp.concatenate(
        [
            real_part[:, :half_cols] - imag_part[:, half_cols:],
            real_part[:, half_cols:] + imag_part[:, :half_cols],
        ],
        axis=1,
    )


def fold_rows(matrix, rows_in):
    return complex_apply(matrix, rows_in)


def per_device(source, forward_mult, schur_inverse, upper_mult):
    local_src = source[0]
    forward_local = forward_mult[0]
    inverse_local = schur_inverse[0]
    upper_local = upper_mult[0]
    sections = lax.axis_size("sect")
    src_float = local_src.astype(jnp.float32)

    def forward_segment(segment_no, current):
        inflow = from_behind(current, "sect", 1)
        summed = fold_rows(forward_local, lax.all_gather(inflow, "slab", axis=0, tiled=True))
        return (src_float + summed).astype(jnp.bfloat16)

    forward_rows = lax.fori_loop(0, sections, forward_segment, local_src)
    scaled = fold_rows(inverse_local, lax.all_gather(forward_rows, "slab", axis=0, tiled=True))

    def backward_segment(segment_no, current):
        outflow = from_behind(current, "sect", -1)
        summed = fold_rows(upper_local, lax.all_gather(outflow, "slab", axis=0, tiled=True))
        return (scaled - summed).astype(jnp.bfloat16)

    wave_rows = lax.fori_loop(0, sections, backward_segment, scaled.astype(jnp.bfloat16))
    return wave_rows[None]


def solution(mesh):
    in_specs = (
        P(("energy", "sect"), "slab", None),
        P(("energy", "sect"), None, "slab", None),
        P(("energy", "sect"), None, "slab", None),
        P(("energy", "sect"), None, "slab", None),
    )
    out_specs = P(("energy", "sect"), "slab", None)
    return jax.shard_map(
        per_device, mesh=mesh, in_specs=in_specs, out_specs=out_specs, check_vma=False
    )
```

profile of v0, /device:TPU:0, one launch (start us, length us, event | category | flops | bytes accessed | tf_op | source)
XLA Modules:
  0.0 181.1 jit_solution(12969878950898552480)
XLA Ops:
  0.0 0.7 copy.19
  0.7 74.7 %while.20 = (s32[]{:T(128)}, bf16[64,128]{1,0:T(8,128)(2,1)S(1)}, bf16[2,64,512]{2,1,0:T(8,128)(2,1)}, f32[64,128]{1,0:T(8,128)S(1)}, s32[]{:T(128)}) while((s32[]{:T(128)}, bf16[64,128]{1,0:T(8,128)(2,1)S(1)}, bf16[2,64,512]{2,1,0:T(8,128)(2,1)}, f32[64,128]{1,0:T(8,128)S(1)}, s32[]{:T(128)}) %tuple.47), condition=%wide.region_1.0_spmd, body=%wide.region_0.0_spmd.sunk | while | flops 16809984 | bytes 1376385 | solution.py:43
  0.7 0.0 copy-start
  0.7 5.0 %collective-permute-start = (bf16[64,128]{1,0:T(8,128)(2,1)S(1)}, bf16[64,128]{1,0:T(8,128)(2,1)S(1)}, u32[]{:S(2)}, u32[]{:S(2)}) collective-permute-start(bf16[64,128]{1,0:T(8,128)(2,1)S(1)} %get-tuple-element.139), channel_id=1, source_target_pairs={{0,16},{1,17},{2,18},{3,19},{4,20},{5,21},{6,22},{7,23},{8,24},{9,... | collective-permute-start | bytes 49160 | tf_op jit(solution)/shard_map/while/body/eval_jaxpr/ppermute | solution.py:10
  5.7 1.4 collective-permute-done
  7.2 30.8 %all_gather.12 = bf16[512,128]{1,0:T(8,128)(2,1)S(1)} all-gather(bf16[64,128]{1,0:T(8,128)(2,1)S(1)} %collective-permute-done), channel_id=1, replica_groups=mesh['sect'=2,'slab'=8,'energy'=2] {'slab'}, dimensions={0}, use_global_device_ids=true | all-gather | bytes 147456 | tf_op jit(solution)/shard_map/while/body/eval_jaxpr/all_gather | solution.py:40
  38.0 0.0 copy-done
  38.0 0.2 fusion.44
  38.2 0.2 fusion.43
  38.3 0.1 slice_subtract_fusion.5
  38.4 0.1 fusion.45
  38.5 0.0 copy-start
  38.5 4.4 %collective-permute-start = (bf16[64,128]{1,0:T(8,128)(2,1)S(1)}, bf16[64,128]{1,0:T(8,128)(2,1)S(1)}, u32[]{:S(2)}, u32[]{:S(2)}) collective-permute-start(bf16[64,128]{1,0:T(8,128)(2,1)S(1)} %get-tuple-element.139), channel_id=1, source_target_pairs={{0,16},{1,17},{2,18},{3,19},{4,20},{5,21},{6,22},{7,23},{8,24},{9,... | collective-permute-start | bytes 49160 | tf_op jit(solution)/shard_map/while/body/eval_jaxpr/ppermute | solution.py:10
  42.9 1.4 collective-permute-done
  44.3 30.6 %all_gather.12 = bf16[512,128]{1,0:T(8,128)(2,1)S(1)} all-gather(bf16[64,128]{1,0:T(8,128)(2,1)S(1)} %collective-permute-done), channel_id=1, replica_groups=mesh['sect'=2,'slab'=8,'energy'=2] {'slab'}, dimensions={0}, use_global_device_ids=true | all-gather | bytes 147456 | tf_op jit(solution)/shard_map/while/body/eval_jaxpr/all_gather | solution.py:40
  74.9 0.0 copy-done
  74.9 0.2 fusion.44
  75.1 0.2 fusion.43
  75.2 0.1 slice_subtract_fusion.5
  75.3 0.1 fusion.45
  75.4 0.0 copy-start.2
  75.4 30.7 %all_gather.9 = bf16[512,128]{1,0:T(8,128)(2,1)S(1)} all-gather(bf16[64,128]{1,0:T(8,128)(2,1)S(1)} %get-tuple-element.49), channel_id=1, replica_groups=mesh['sect'=2,'slab'=8,'energy'=2] {'slab'}, dimensions={0}, use_global_device_ids=true | all-gather | bytes 147456 | tf_op jit(solution)/shard_map/all_gather | solution.py:44
  106.1 0.0 copy-done.2
  106.1 0.2 convolution_bitcast_fusion.1
  106.2 0.2 convolution_bitcast_fusion
  106.4 0.0 copy-start.1
  106.4 0.1 slice_subtract_fusion.2
  106.5 0.1 fusion.18
  106.6 0.7 copy-done.1
  107.3 73.2 %while.21 = (s32[]{:T(128)}, bf16[64,128]{1,0:T(8,128)(2,1)S(1)}, bf16[2,64,512]{2,1,0:T(8,128)(2,1)S(1)}, f32[64,128]{1,0:T(8,128)S(1)}, s32[]{:T(128)}) while((s32[]{:T(128)}, bf16[64,128]{1,0:T(8,128)(2,1)S(1)}, bf16[2,64,512]{2,1,0:T(8,128)(2,1)S(1)}, f32[64,128]{1,0:T(8,128)S(1)}, s32[]{:T(128)}) %tuple.46), condition=%wide.region_3.0_spmd, body=%wide.region_2.0_spmd.sunk | while | flops 16809984 | bytes 852069 | solution.py:51
  107.3 1.3 collective-permute-start.1
  108.6 4.3 %collective-permute-done.1 = bf16[64,128]{1,0:T(8,128)(2,1)S(1)} collective-permute-done((bf16[64,128]{1,0:T(8,128)(2,1)S(1)}, bf16[64,128]{1,0:T(8,128)(2,1)S(1)}, u32[]{:S(2)}, u32[]{:S(2)}) %collective-permute-start.1) | collective-permute-done | bytes 16416 | tf_op jit(solution)/shard_map/while/body/eval_jaxpr/ppermute | solution.py:10
  112.9 30.5 %all_gather.13 = bf16[512,128]{1,0:T(8,128)(2,1)S(1)} all-gather(bf16[64,128]{1,0:T(8,128)(2,1)S(1)} %collective-permute-done.1), channel_id=1, replica_groups=mesh['sect'=2,'slab'=8,'energy'=2] {'slab'}, dimensions={0}, use_global_device_ids=true | all-gather | bytes 147456 | tf_op jit(solution)/shard_map/while/body/eval_jaxpr/all_gather | solution.py:48
  143.4 0.2 fusion.51
  143.6 0.2 fusion.50
  143.7 0.1 slice_subtract_fusion.6
  143.8 0.1 fusion.52
  143.9 1.3 collective-permute-start.1
  145.2 4.3 %collective-permute-done.1 = bf16[64,128]{1,0:T(8,128)(2,1)S(1)} collective-permute-done((bf16[64,128]{1,0:T(8,128)(2,1)S(1)}, bf16[64,128]{1,0:T(8,128)(2,1)S(1)}, u32[]{:S(2)}, u32[]{:S(2)}) %collective-permute-start.1) | collective-permute-done | bytes 16416 | tf_op jit(solution)/shard_map/while/body/eval_jaxpr/ppermute | solution.py:10
  149.5 30.5 %all_gather.13 = bf16[512,128]{1,0:T(8,128)(2,1)S(1)} all-gather(bf16[64,128]{1,0:T(8,128)(2,1)S(1)} %collective-permute-done.1), channel_id=1, replica_groups=mesh['sect'=2,'slab'=8,'energy'=2] {'slab'}, dimensions={0}, use_global_device_ids=true | all-gather | bytes 147456 | tf_op jit(solution)/shard_map/while/body/eval_jaxpr/all_gather | solution.py:48
  180.1 0.2 fusion.51
  180.2 0.2 fusion.50
  180.4 0.1 slice_subtract_fusion.6
  180.5 0.1 fusion.52
  180.5 0.0 copy-start.3
  180.5 0.6 copy-done.3
  (1 shorter events, 0.0 us)
Async XLA Ops:
  0.7 37.3 %copy-start = (bf16[2,64,512]{2,1,0:T(8,128)(2,1)S(1)}, bf16[2,64,512]{2,1,0:T(8,128)(2,1)}, u32[]{:S(2)}) copy-start(bf16[2,64,512]{2,1,0:T(8,128)(2,1)} %get-tuple-element.145) | copy-start | bytes 393220 | tf_op jit(solution)/shard_map/while
  0.7 6.4 %collective-permute-start = (bf16[64,128]{1,0:T(8,128)(2,1)S(1)}, bf16[64,128]{1,0:T(8,128)(2,1)S(1)}, u32[]{:S(2)}, u32[]{:S(2)}) collective-permute-start(bf16[64,128]{1,0:T(8,128)(2,1)S(1)} %get-tuple-element.139), channel_id=1, source_target_pairs={{0,16},{1,17},{2,18},{3,19},{4,20},{5,21},{6,22},{7,23},{8,24},{9,... | collective-permute-start | bytes 49160 | tf_op jit(solution)/shard_map/while/body/eval_jaxpr/ppermute | solution.py:10
  38.5 36.4 %copy-start = (bf16[2,64,512]{2,1,0:T(8,128)(2,1)S(1)}, bf16[2,64,512]{2,1,0:T(8,128)(2,1)}, u32[]{:S(2)}) copy-start(bf16[2,64,512]{2,1,0:T(8,128)(2,1)} %get-tuple-element.145) | copy-start | bytes 393220 | tf_op jit(solution)/shard_map/while
  38.5 5.8 %collective-permute-start = (bf16[64,128]{1,0:T(8,128)(2,1)S(1)}, bf16[64,128]{1,0:T(8,128)(2,1)S(1)}, u32[]{:S(2)}, u32[]{:S(2)}) collective-permute-start(bf16[64,128]{1,0:T(8,128)(2,1)S(1)} %get-tuple-element.139), channel_id=1, source_target_pairs={{0,16},{1,17},{2,18},{3,19},{4,20},{5,21},{6,22},{7,23},{8,24},{9,... | collective-permute-start | bytes 49160 | tf_op jit(solution)/shard_map/while/body/eval_jaxpr/ppermute | solution.py:10
  75.4 30.7 %copy-start.2 = (bf16[1,2,64,512]{3,2,1,0:T(8,128)(2,1)S(1)}, bf16[1,2,64,512]{3,2,1,0:T(8,128)(2,1)}, u32[]{:S(2)}) copy-start(bf16[1,2,64,512]{3,2,1,0:T(8,128)(2,1)} %param.10) | copy-start | bytes 393220
  106.4 0.9 copy-start.1
  107.3 5.6 %collective-permute-start.1 = (bf16[64,128]{1,0:T(8,128)(2,1)S(1)}, bf16[64,128]{1,0:T(8,128)(2,1)S(1)}, u32[]{:S(2)}, u32[]{:S(2)}) collective-permute-start(bf16[64,128]{1,0:T(8,128)(2,1)S(1)} %get-tuple-element.154), channel_id=1, source_target_pairs={{16,0},{17,1},{18,2},{19,3},{20,4},{21,5},{22,6},{23,7},{24,8},{25... | collective-permute-start | bytes 49160 | tf_op jit(solution)/shard_map/while/body/eval_jaxpr/ppermute | solution.py:10
  143.9 5.6 %collective-permute-start.1 = (bf16[64,128]{1,0:T(8,128)(2,1)S(1)}, bf16[64,128]{1,0:T(8,128)(2,1)S(1)}, u32[]{:S(2)}, u32[]{:S(2)}) collective-permute-start(bf16[64,128]{1,0:T(8,128)(2,1)S(1)} %get-tuple-element.154), channel_id=1, source_target_pairs={{16,0},{17,1},{18,2},{19,3},{20,4},{21,5},{22,6},{23,7},{24,8},{25... | collective-permute-start | bytes 49160 | tf_op jit(solution)/shard_map/while/body/eval_jaxpr/ppermute | solution.py:10
  180.5 0.6 copy-start.3
where the time goes:
time: 181 us
  blocking collectives  153 us (85%)
  starting transfers between devices  12 us (7%)
  waiting for transfers between devices  11.5 us (6%)
  local copies, waits for them, and re-layouts  2.07 us (1%)
    all_gather x2, blocking collectives, forward_segment(): lax.all_gather(inflow, 'slab', axis=0, tiled=True)  61.4 us
    all_gather x2, blocking collectives, backward_segment(): lax.all_gather(outflow, 'slab', axis=0, tiled=True)  61 us
    all_gather x1, blocking collectives, per_device(): lax.all_gather(forward_rows, 'slab', axis=0, tiled=True)  30.7 us
    ppermute x4, starting transfers between devices, from_behind(): return lax.ppermute(block, axis, route)  12 us
    ppermute x4, waiting for transfers between devices, from_behind(): return lax.ppermute(block, axis, route)  11.5 us
  transfers between devices with their start and end apart: 4, of which 4 were waited for; matrix products, arithmetic and copies ran while one was open for 0% of the time, Pallas kernels for 0%

commit v1 on v0

v1 whole, which is shorter than its diff:
```python
import jax
import jax.numpy as jnp
from jax import lax
from jax.sharding import PartitionSpec as P


def from_behind(block, axis, distance):
    devices = range(lax.axis_size(axis))
    route = [(i - distance, i) for i in devices if i - distance in devices]
    return lax.ppermute(block, axis, route)


def gather_rows(rows):
    devices = lax.axis_size("slab")
    copies = jnp.broadcast_to(rows[None], (devices,) + rows.shape)
    blocks = lax.all_to_all(copies, "slab", split_axis=0, concat_axis=0)
    return blocks.reshape((devices * rows.shape[0],) + rows.shape[1:])


def complex_apply(matrix, vector):
    rows, half_cols = matrix.shape[0] // 2, vector.shape[1] // 2
    both = jnp.dot(matrix, vector, preferred_element_type=jnp.float32)
    real_part, imag_part = both[:rows], both[rows:]
    return jnp.concatenate(
        [
            real_part[:, :half_cols] - imag_part[:, half_cols:],
            real_part[:, half_cols:] + imag_part[:, :half_cols],
        ],
        axis=1,
    )


def two_sections(src, forward, inverse, upper):
    first = lax.axis_index("sect") == 0
    height, order = forward.shape
    flat = src.reshape(-1, order)
    bundle = jnp.concatenate([forward, inverse, flat], axis=0)
    other = lax.ppermute(bundle, "sect", [(0, 1), (1, 0)])
    src_all = gather_rows(src)
    other_forward, other_inverse = other[:height], other[height : 2 * height]
    other_src = other[2 * height :].reshape(src.shape)

    next_forward = (other_src.astype(jnp.float32) + complex_apply(other_forward, src_all)).astype(jnp.bfloat16)
    scaled = complex_apply(inverse, src_all)

    second = gather_rows(jnp.where(first, next_forward, other_src))
    matrix = jnp.where(first, other_inverse, forward)
    added = jnp.where(first, jnp.zeros_like(src), src).astype(jnp.float32)
    rows = (added + complex_apply(matrix, second)).astype(jnp.bfloat16)

    third = gather_rows(rows)
    matrix = jnp.where(first, upper, inverse)
    product = complex_apply(matrix, third)
    return jnp.where(first, scaled - product, product).astype(jnp.bfloat16)


def many_sections(src, forward, inverse, upper):
    sections = lax.axis_size("sect")
    src_float = src.astype(jnp.float32)

    def forward_segment(segment_no, current):
        inflow = from_behind(current, "sect", 1)
        return (src_float + complex_apply(forward, gather_rows(inflow))).astype(jnp.bfloat16)

    forward_rows = lax.fori_loop(1, sections, forward_segment, src)
    scaled = complex_apply(inverse, gather_rows(forward_rows))

    def backward_segment(segment_no, current):
        outflow = from_behind(current, "sect", -1)
        return (scaled - complex_apply(upper, gather_rows(outflow))).astype(jnp.bfloat16)

    return lax.fori_loop(1, sections, backward_segment, scaled.astype(jnp.bfloat16))


def per_device(source, forward_mult, schur_inverse, upper_mult):
    src = source[0]
    forward, inverse, upper = (m[0].reshape(-1, m.shape[-1]) for m in (forward_mult, schur_inverse, upper_mult))
    fits = src.size % forward.shape[-1] == 0
    run = two_sections if lax.axis_size("sect") == 2 and fits else many_sections
    return run(src, forward, inverse, upper)[None]


def solution(mesh):
    in_specs = (
        P(("energy", "sect"), "slab", None),
        P(("energy", "sect"), None, "slab", None),
        P(("energy", "sect"), None, "slab", None),
        P(("energy", "sect"), None, "slab", None),
    )
    out_specs = P(("energy", "sect"), "slab", None)
    return jax.shard_map(
        per_device, mesh=mesh, in_specs=in_specs, out_specs=out_specs, check_vma=False
    )
```

time: 181 us -> 43.7 us (0.24)
  blocking collectives: 153 us -> 0 us
  waiting for transfers between devices: 11.5 us -> 21.6 us
  starting transfers between devices: 12 us -> 15.7 us
    all_gather x5 -> x0, blocking collectives: 153 us -> none  [the longest x2 61.4 us: forward_segment(): lax.all_gather(inflow, 'slab', axis=0, tiled=True)]
    all_to_all x0 -> x3, waiting for transfers between devices: none -> 21.6 us  [gather_rows(): blocks = lax.all_to_all(copies, 'slab', split_axis=0, concat_axis=0)]
    all_to_all x0 -> x3, starting transfers between devices: none -> 12.7 us  [gather_rows(): blocks = lax.all_to_all(copies, 'slab', split_axis=0, concat_axis=0)]
    ppermute x4 -> x1, waiting for transfers between devices: 11.5 us -> 0.01 us  [two_sections(): other = lax.ppermute(bundle, 'sect', [(0, 1), (1, 0)])]
    ppermute x4 -> x1, starting transfers between devices: 12 us -> 3.03 us  [two_sections(): other = lax.ppermute(bundle, 'sect', [(0, 1), (1, 0)])]
    unnamed x7 -> x8, local copies, waits for them, and re-layouts: 2.06 us -> 0.02 us
    broadcast_in_dim x0 -> x3, local copies, waits for them, and re-layouts: none -> 2.01 us  [gather_rows(): copies = jnp.broadcast_to(rows[None], (devices,) + rows.shape)]
  transfers between devices with their start and end apart: 4 -> 4, of which waited for: 4 -> 3; matrix products, arithmetic and copies ran while one was open for 0% -> 2% of each run, Pallas kernels for 0% -> 0%
where the time goes in v1:
time: 43.7 us; the launch traced here: 43.1 us
  waiting for transfers between devices  21.6 us (49%)
  starting transfers between devices  15.7 us (36%)
  local copies, waits for them, and re-layouts  2.79 us (6%)
  other arithmetic  2.2 us (5%)
  matrix products  0.69 us (2%)
    all_to_all x3, waiting for transfers between devices, gather_rows(): blocks = lax.all_to_all(copies, 'slab', split_axis=0, concat_axis=0)  21.6 us
    all_to_all x3, starting transfers between devices, gather_rows(): blocks = lax.all_to_all(copies, 'slab', split_axis=0, concat_axis=0)  12.7 us
    ppermute x1, starting transfers between devices, two_sections(): other = lax.ppermute(bundle, 'sect', [(0, 1), (1, 0)])  3.03 us
    broadcast_in_dim x3, local copies, waits for them, and re-layouts, gather_rows(): copies = jnp.broadcast_to(rows[None], (devices,) + rows.shape)  2.01 us
    concatenate x1, other arithmetic, two_sections(): bundle = jnp.concatenate([forward, inverse, flat], axis=0)  0.99 us
  transfers between devices with their start and end apart: 4, of which 3 were waited for; matrix products, arithmetic and copies ran while one was open for 2% of the time, Pallas kernels for 0%

profile of v1, /device:TPU:0, one launch (start us, length us, event | category | flops | bytes accessed | tf_op | source)
XLA Modules:
  0.0 43.1 jit_solution(15826956119842449790)
XLA Ops:
  0.0 0.7 %reshape_squeeze.12 = bf16[16,512]{1,0:T(8,128)(2,1)S(1)} reshape(bf16[1,64,128]{2,1,0:T(8,128)(2,1)} %param.4) | data formatting | bytes 32768 | tf_op jit(solution)/shard_map/reshape;squeeze | solution.py:36
  0.7 0.0 copy-start.2
  0.8 1.0 %pad_maximum_fusion = bf16[272,512]{1,0:T(8,128)(2,1)S(1)} fusion(bf16[16,512]{1,0:T(8,128)(2,1)S(1)} %reshape_squeeze.12, bf16[128,512]{1,0:T(8,128)(2,1)} %bitcast.27, bf16[128,512]{1,0:T(8,128)(2,1)} %bitcast.31), kind=kLoop, calls=%fused_computation | loop fusion | flops 835584 | bytes 557056 | tf_op jit(solution)/shard_map/concatenate | solution.py:37
  1.7 3.0 %collective-permute-start = (bf16[272,512]{1,0:T(8,128)(2,1)S(1)}, bf16[272,512]{1,0:T(8,128)(2,1)S(1)}, u32[]{:S(2)}, u32[]{:S(2)}) collective-permute-start(bf16[272,512]{1,0:T(8,128)(2,1)S(1)} %pad_maximum_fusion), channel_id=1, source_target_pairs={{0,16},{16,0},{1,17},{17,1},{2,18},{18,2},{3,19},{19,3},{4,20},{20... | collective-permute-start | bytes 835592 | tf_op jit(solution)/shard_map/ppermute | solution.py:38
  4.8 0.0 copy-done.2
  4.8 0.7 %broadcast_in_dim.26 = bf16[8,64,128]{2,1,0:T(8,128)(2,1)} broadcast(bf16[64,128]{1,0:T(8,128)(2,1)S(1)} %bitcast.36), dimensions={1,2} | broadcast | bytes 147456 | tf_op jit(solution)/shard_map/broadcast_in_dim | solution.py:15
  5.5 5.8 %all-to-all-start = ((bf16[8,64,128]{2,1,0:T(8,128)(2,1)}), bf16[8,64,128]{2,1,0:T(8,128)(2,1)S(1)}, u32[]{:S(2)}, u32[]{:S(2)}) async-start(bf16[8,64,128]{2,1,0:T(8,128)(2,1)} %broadcast_in_dim.26), calls=%async_computation | async-start | bytes 262144 | tf_op jit(solution)/shard_map/all_to_all | solution.py:16
  11.3 7.3 %all-to-all-done = bf16[8,64,128]{2,1,0:T(8,128)(2,1)S(1)} async-done(((bf16[8,64,128]{2,1,0:T(8,128)(2,1)}), bf16[8,64,128]{2,1,0:T(8,128)(2,1)S(1)}, u32[]{:S(2)}, u32[]{:S(2)}) %all-to-all-start) | async-done | bytes 131104 | tf_op jit(solution)/shard_map/all_to_all | solution.py:16
  18.6 0.0 collective-permute-done
  18.6 0.2 fusion
  18.8 0.1 slice_subtract_fusion.2
  18.9 0.1 fusion.13
  19.0 0.7 %broadcast_in_dim.28 = bf16[8,64,128]{2,1,0:T(8,128)(2,1)} broadcast(bf16[64,128]{1,0:T(8,128)(2,1)S(1)} %fusion.13), dimensions={1,2} | broadcast | bytes 147456 | tf_op jit(solution)/shard_map/broadcast_in_dim | solution.py:15
  19.7 0.0 copy-start
  19.7 0.0 copy-start.3
  19.7 3.5 %all-to-all-start.1 = ((bf16[8,64,128]{2,1,0:T(8,128)(2,1)}), bf16[8,64,128]{2,1,0:T(8,128)(2,1)S(1)}, u32[]{:S(2)}, u32[]{:S(2)}) async-start(bf16[8,64,128]{2,1,0:T(8,128)(2,1)} %broadcast_in_dim.28), calls=%async_computation.1 | async-start | bytes 262144 | tf_op jit(solution)/shard_map/all_to_all | solution.py:16
  23.2 0.0 copy-done
  23.2 0.0 copy-done.3
  23.2 0.0 copy-start.1
  23.3 7.2 %all-to-all-done.1 = bf16[8,64,128]{2,1,0:T(8,128)(2,1)S(1)} async-done(((bf16[8,64,128]{2,1,0:T(8,128)(2,1)}), bf16[8,64,128]{2,1,0:T(8,128)(2,1)S(1)}, u32[]{:S(2)}, u32[]{:S(2)}) %all-to-all-start.1) | async-done | bytes 131104 | tf_op jit(solution)/shard_map/all_to_all | solution.py:16
  30.5 0.0 copy-done.1
  30.5 0.2 fusion.2
  30.7 0.1 fusion.8
  30.8 0.1 fusion.14
  30.8 0.7 %broadcast_in_dim.30 = bf16[8,64,128]{2,1,0:T(8,128)(2,1)} broadcast(bf16[64,128]{1,0:T(8,128)(2,1)S(1)} %fusion.14), dimensions={1,2} | broadcast | bytes 147456 | tf_op jit(solution)/shard_map/broadcast_in_dim | solution.py:15
  31.5 3.4 %all-to-all-start.2 = ((bf16[8,64,128]{2,1,0:T(8,128)(2,1)}), bf16[8,64,128]{2,1,0:T(8,128)(2,1)S(1)}, u32[]{:S(2)}, u32[]{:S(2)}) async-start(bf16[8,64,128]{2,1,0:T(8,128)(2,1)} %broadcast_in_dim.30), calls=%async_computation.2 | async-start | bytes 262144 | tf_op jit(solution)/shard_map/all_to_all | solution.py:16
  34.9 0.2 fusion.15
  35.1 0.1 fusion.10
  35.2 7.0 %all-to-all-done.2 = bf16[8,64,128]{2,1,0:T(8,128)(2,1)S(1)} async-done(((bf16[8,64,128]{2,1,0:T(8,128)(2,1)}), bf16[8,64,128]{2,1,0:T(8,128)(2,1)S(1)}, u32[]{:S(2)}, u32[]{:S(2)}) %all-to-all-start.2) | async-done | bytes 131104 | tf_op jit(solution)/shard_map/all_to_all | solution.py:16
  42.2 0.2 fusion.16
  42.4 0.1 fusion.6
  42.4 0.7 %fusion.4 = bf16[1,64,128]{2,1,0:T(8,128)(2,1)} fusion(f32[1,64,64]{2,1,0:T(8,128)S(1)} %get-tuple-element.12, f32[1,64,64]{2,1,0:T(8,128)S(1)} %get-tuple-element.11, f32[1,64,64]{2,1,0:T(8,128)S(1)} %get-tuple-element.6, f32[1,64,64]{2,1,0:T(8,128)S(1)} %get-tuple-element.5, pred[]{:T(512)S(6)} %eq.3), kind=kLoop, calls=%fused_computation.8 | loop fusion | flops 40960 | bytes 81921 | tf_op jit(solution)/shard_map/convert_element_type | solution.py:54
  (3 shorter events, 0.0 us)
Async XLA Ops:
  0.7 4.0 %copy-start.2 = (bf16[1,64,128]{2,1,0:T(8,128)(2,1)S(1)}, bf16[1,64,128]{2,1,0:T(8,128)(2,1)}, u32[]{:S(2)}) copy-start(bf16[1,64,128]{2,1,0:T(8,128)(2,1)} %param.4) | copy-start | bytes 49156
  1.7 16.9 %collective-permute-start = (bf16[272,512]{1,0:T(8,128)(2,1)S(1)}, bf16[272,512]{1,0:T(8,128)(2,1)S(1)}, u32[]{:S(2)}, u32[]{:S(2)}) collective-permute-start(bf16[272,512]{1,0:T(8,128)(2,1)S(1)} %pad_maximum_fusion), channel_id=1, source_target_pairs={{0,16},{16,0},{1,17},{17,1},{2,18},{18,2},{3,19},{19,3},{4,20},{20... | collective-permute-start | bytes 835592 | tf_op jit(solution)/shard_map/ppermute | solution.py:38
  5.5 13.2 %all-to-all-start = ((bf16[8,64,128]{2,1,0:T(8,128)(2,1)}), bf16[8,64,128]{2,1,0:T(8,128)(2,1)S(1)}, u32[]{:S(2)}, u32[]{:S(2)}) async-start(bf16[8,64,128]{2,1,0:T(8,128)(2,1)} %broadcast_in_dim.26), calls=%async_computation | async-start | bytes 262144 | tf_op jit(solution)/shard_map/all_to_all | solution.py:16
  19.7 3.5 %copy-start = (bf16[1,2,64,512]{3,2,1,0:T(8,128)(2,1)S(1)}, bf16[1,2,64,512]{3,2,1,0:T(8,128)(2,1)}, u32[]{:S(2)}) copy-start(bf16[1,2,64,512]{3,2,1,0:T(8,128)(2,1)} %param.6) | copy-start | bytes 393220
  19.7 3.5 %copy-start.3 = (bf16[1,2,64,512]{3,2,1,0:T(8,128)(2,1)S(1)}, bf16[1,2,64,512]{3,2,1,0:T(8,128)(2,1)}, u32[]{:S(2)}) copy-start(bf16[1,2,64,512]{3,2,1,0:T(8,128)(2,1)} %param.7) | copy-start | bytes 393220
  19.7 10.8 %all-to-all-start.1 = ((bf16[8,64,128]{2,1,0:T(8,128)(2,1)}), bf16[8,64,128]{2,1,0:T(8,128)(2,1)S(1)}, u32[]{:S(2)}, u32[]{:S(2)}) async-start(bf16[8,64,128]{2,1,0:T(8,128)(2,1)} %broadcast_in_dim.28), calls=%async_computation.1 | async-start | bytes 262144 | tf_op jit(solution)/shard_map/all_to_all | solution.py:16
  23.2 7.3 %copy-start.1 = (bf16[1,2,64,512]{3,2,1,0:T(8,128)(2,1)S(1)}, bf16[1,2,64,512]{3,2,1,0:T(8,128)(2,1)}, u32[]{:S(2)}) copy-start(bf16[1,2,64,512]{3,2,1,0:T(8,128)(2,1)} %param.5) | copy-start | bytes 393220
  31.5 10.7 %all-to-all-start.2 = ((bf16[8,64,128]{2,1,0:T(8,128)(2,1)}), bf16[8,64,128]{2,1,0:T(8,128)(2,1)S(1)}, u32[]{:S(2)}, u32[]{:S(2)}) async-start(bf16[8,64,128]{2,1,0:T(8,128)(2,1)} %broadcast_in_dim.30), calls=%async_computation.2 | async-start | bytes 262144 | tf_op jit(solution)/shard_map/all_to_all | solution.py:16

commit v2 on v1

--- a/solution.py
+++ b/solution.py
@@ -12,12 +12,15 @@
 
 def gather_rows(rows):
     devices = lax.axis_size("slab")
+    middle = devices // 2 + 1 if devices > 2 else 0
+    order = [(middle - i) % devices for i in range(devices)]
     copies = jnp.broadcast_to(rows[None], (devices,) + rows.shape)
-    blocks = lax.all_to_all(copies, "slab", split_axis=0, concat_axis=0)
-    return blocks.reshape((devices * rows.shape[0],) + rows.shape[1:])
+    blocks = lax.all_to_all(copies, "slab", split_axis=0, concat_axis=0, axis_index_groups=[order])
+    return [blocks[order.index(i)] for i in range(devices)]
 
 
-def complex_apply(matrix, vector):
+def complex_apply(matrix, blocks):
+    vector = jnp.concatenate(blocks, axis=0)
     rows, half_cols = matrix.shape[0] // 2, vector.shape[1] // 2
     both = jnp.dot(matrix, vector, preferred_element_type=jnp.float32)
     real_part, imag_part = both[:rows], both[rows:]
@@ -31,27 +34,32 @@
 
 
 def two_sections(src, forward, inverse, upper):
+    swap = [(0, 1), (1, 0)]
     first = lax.axis_index("sect") == 0
-    height, order = forward.shape
-    flat = src.reshape(-1, order)
-    bundle = jnp.concatenate([forward, inverse, flat], axis=0)
-    other = lax.ppermute(bundle, "sect", [(0, 1), (1, 0)])
-    src_all = gather_rows(src)
-    other_forward, other_inverse = other[:height], other[height : 2 * height]
-    other_src = other[2 * height :].reshape(src.shape)
+    other_forward = lax.ppermute(forward, "sect", swap)
+    other_src = lax.ppermute(src, "sect", swap)
+    other_inverse = lax.ppermute(inverse, "sect", swap)
+    src_blocks = gather_rows(src)
+    last = jnp.where(
+        first,
+        jnp.concatenate([inverse, -upper], axis=1),
+        jnp.concatenate([jnp.zeros_like(inverse), inverse], axis=1),
+    )
+    mine = jnp.where(first, jnp.zeros_like(forward), forward)
+    added = jnp.where(first, jnp.zeros_like(src), src).astype(jnp.float32)
+    other_forward, other_src, src_blocks, last, mine, added = lax.optimization_barrier(
+        (other_forward, other_src, src_blocks, last, mine, added)
+    )
 
-    next_forward = (other_src.astype(jnp.float32) + complex_apply(other_forward, src_all)).astype(jnp.bfloat16)
-    scaled = complex_apply(inverse, src_all)
+    next_forward = (other_src.astype(jnp.float32) + complex_apply(other_forward, src_blocks)).astype(jnp.bfloat16)
+    second = gather_rows(jnp.where(first, next_forward, other_src))
 
-    second = gather_rows(jnp.where(first, next_forward, other_src))
-    matrix = jnp.where(first, other_inverse, forward)
-    added = jnp.where(first, jnp.zeros_like(src), src).astype(jnp.float32)
+    other_inverse, second = lax.optimization_barrier((other_inverse, second))
+    matrix = jnp.where(first, other_inverse, mine)
     rows = (added + complex_apply(matrix, second)).astype(jnp.bfloat16)
 
     third = gather_rows(rows)
-    matrix = jnp.where(first, upper, inverse)
-    product = complex_apply(matrix, third)
-    return jnp.where(first, scaled - product, product).astype(jnp.bfloat16)
+    return complex_apply(last, src_blocks + third).astype(jnp.bfloat16)
 
 
 def many_sections(src, forward, inverse, upper):
@@ -75,8 +83,7 @@
 def per_device(source, forward_mult, schur_inverse, upper_mult):
     src = source[0]
     forward, inverse, upper = (m[0].reshape(-1, m.shape[-1]) for m in (forward_mult, schur_inverse, upper_mult))
-    fits = src.size % forward.shape[-1] == 0
-    run = two_sections if lax.axis_size("sect") == 2 and fits else many_sections
+    run = two_sections if lax.axis_size("sect") == 2 else many_sections
     return run(src, forward, inverse, upper)[None]
 
 

time: 43.7 us -> 38.1 us (0.87)
  waiting for transfers between devices: 21.6 us -> 7.82 us
  blocking collectives: 0 us -> 8.45 us
  other arithmetic: 2.2 us -> 1.2 us
  local copies, waits for them, and re-layouts: 2.79 us -> 3.23 us
    all_to_all x3 -> x2, waiting for transfers between devices: 21.6 us -> 5.16 us  [gather_rows(): lax.all_to_all(copies, 'slab', split_axis=0, concat_axis=0, axis_index_gr...]
    all_to_all x0 -> x1, blocking collectives: none -> 8.45 us  [gather_rows(): lax.all_to_all(copies, 'slab', split_axis=0, concat_axis=0, axis_index_gr...]
    ppermute x1 -> x3, waiting for transfers between devices: 0.01 us -> 2.66 us  [the longest x1 1.39 us: two_sections(): other_inverse = lax.ppermute(inverse, 'sect', swap)]
    unnamed x8 -> x29, local copies, waits for them, and re-layouts: 0.02 us -> 1.07 us
    ppermute x1 -> x3, starting transfers between devices: 3.03 us -> 4.04 us  [the longest x1 2.97 us: two_sections(): other_src = lax.ppermute(src, 'sect', swap)]
    concatenate x1 -> x0, other arithmetic: 0.99 us -> none  [two_sections(): bundle = jnp.concatenate([forward, inverse, flat], axis=0)]
    another operation x1 -> x0, local copies, waits for them, and re-layouts: 0.74 us -> none  [two_sections(): flat = src.reshape(-1, order)]
    all_to_all x3 -> x2, starting transfers between devices: 12.7 us -> 12.1 us  [gather_rows(): lax.all_to_all(copies, 'slab', split_axis=0, concat_axis=0, axis_index_gr...]
  transfers between devices with their start and end apart: 4 -> 5, of which waited for: 3 -> 4; matrix products, arithmetic and copies ran while one was open for 2% -> 4% of each run, Pallas kernels for 0% -> 0%
where the time goes in v2:
time: 38.1 us; the launch traced here: 37.5 us
  starting transfers between devices  16.1 us (42%)
  blocking collectives  8.45 us (22%)
  waiting for transfers between devices  7.82 us (21%)
  local copies, waits for them, and re-layouts  3.23 us (8%)
  other arithmetic  1.2 us (3%)
  matrix products  0.56 us (1%)
    all_to_all x2, starting transfers between devices, gather_rows(): lax.all_to_all(copies, 'slab', split_axis=0, concat_axis=0, axis_index_gr...  12.1 us
    all_to_all x1, blocking collectives, gather_rows(): lax.all_to_all(copies, 'slab', split_axis=0, concat_axis=0, axis_index_gr...  8.45 us
    all_to_all x2, waiting for transfers between devices, gather_rows(): lax.all_to_all(copies, 'slab', split_axis=0, concat_axis=0, axis_index_gr...  5.16 us
    ppermute x1, starting transfers between devices, two_sections(): other_src = lax.ppermute(src, 'sect', swap)  2.97 us
    broadcast_in_dim x3, local copies, waits for them, and re-layouts, gather_rows(): copies = jnp.broadcast_to(rows[None], (devices,) + rows.shape)  2.11 us
    ppermute x1, waiting for transfers between devices, two_sections(): other_inverse = lax.ppermute(inverse, 'sect', swap)  1.39 us
    ppermute x1, waiting for transfers between devices, two_sections(): other_forward = lax.ppermute(forward, 'sect', swap)  1.26 us
    unnamed x29, local copies, waits for them, and re-layouts  1.07 us
  transfers between devices with their start and end apart: 5, of which 4 were waited for; matrix products, arithmetic and copies ran while one was open for 4% of the time, Pallas kernels for 0%

profile of v2, /device:TPU:0, one launch (start us, length us, event | category | flops | bytes accessed | tf_op | source)
XLA Modules:
  0.0 37.5 jit_solution(16730427144475390170)
XLA Ops:
  0.0 3.0 %collective-permute-start.1 = (bf16[64,128]{1,0:T(8,128)(2,1)}, bf16[64,128]{1,0:T(8,128)(2,1)S(1)}, u32[]{:S(2)}, u32[]{:S(2)}) collective-permute-start(bf16[64,128]{1,0:T(8,128)(2,1)} %bitcast.83), channel_id=1, source_target_pairs={{0,16},{16,0},{1,17},{17,1},{2,18},{18,2},{3,19},{19,3},{4,20},{20... | collective-permute-start | bytes 49160 | tf_op jit(solution)/shard_map/ppermute | solution.py:40
  3.0 1.4 %broadcast_in_dim.8 = bf16[8,64,128]{2,1,0:T(8,128)(2,1)} broadcast(bf16[64,128]{1,0:T(8,128)(2,1)} %bitcast.84), dimensions={1,2} | broadcast | bytes 147456 | tf_op jit(solution)/shard_map/broadcast_in_dim | solution.py:17
  4.4 0.0 copy-start.2
  4.4 0.0 copy-start.1
  4.4 7.0 %all-to-all-start = ((bf16[8,64,128]{2,1,0:T(8,128)(2,1)}), bf16[8,64,128]{2,1,0:T(8,128)(2,1)S(1)}, u32[]{:S(2)}, u32[]{:S(2)}) async-start(bf16[8,64,128]{2,1,0:T(8,128)(2,1)} %broadcast_in_dim.8), calls=%async_computation | async-start | bytes 262144 | tf_op jit(solution)/shard_map/all_to_all | solution.py:18
  11.4 0.0 copy-done.2
  11.4 0.5 %collective-permute-start = (bf16[128,512]{1,0:T(8,128)(2,1)S(1)}, bf16[128,512]{1,0:T(8,128)(2,1)S(1)}, u32[]{:S(2)}, u32[]{:S(2)}) collective-permute-start(bf16[128,512]{1,0:T(8,128)(2,1)S(1)} %bitcast.82), channel_id=1, source_target_pairs={{0,16},{16,0},{1,17},{17,1},{2,18},{18,2},{3,19},{19,3},{4,20},{20... | collective-permute-start | bytes 393224 | tf_op jit(solution)/shard_map/ppermute | solution.py:39
  11.9 0.0 copy-done.1
  11.9 0.0 copy-start.3
  11.9 0.0 copy-start
  11.9 0.7 %copy-done.3 = bf16[1,64,128]{2,1,0:T(8,128)(2,1)S(1)} copy-done((bf16[1,64,128]{2,1,0:T(8,128)(2,1)S(1)}, bf16[1,64,128]{2,1,0:T(8,128)(2,1)}, u32[]{:S(2)}) %copy-start.3) | copy-done | bytes 16408
  12.6 0.2 copy-done
  12.8 0.1 maximum_select_fusion
  12.9 2.1 %all-to-all-done = bf16[8,64,128]{2,1,0:T(8,128)(2,1)S(1)} async-done(((bf16[8,64,128]{2,1,0:T(8,128)(2,1)}), bf16[8,64,128]{2,1,0:T(8,128)(2,1)S(1)}, u32[]{:S(2)}, u32[]{:S(2)}) %all-to-all-start) | async-done | bytes 131104 | tf_op jit(solution)/shard_map/all_to_all | solution.py:18
  15.1 0.0 collective-permute-done.1
  15.1 1.3 %collective-permute-done = bf16[128,512]{1,0:T(8,128)(2,1)S(1)} collective-permute-done((bf16[128,512]{1,0:T(8,128)(2,1)S(1)}, bf16[128,512]{1,0:T(8,128)(2,1)S(1)}, u32[]{:S(2)}, u32[]{:S(2)}) %collective-permute-start) | collective-permute-done | bytes 131104 | tf_op jit(solution)/shard_map/ppermute | solution.py:39
  16.5 0.2 fusion.10
  16.6 0.1 slice_subtract_fusion.2
  16.7 0.1 fusion.7
  16.8 0.7 %broadcast_in_dim.10 = bf16[8,64,128]{2,1,0:T(8,128)(2,1)} broadcast(bf16[64,128]{1,0:T(8,128)(2,1)S(1)} %fusion.7), dimensions={1,2} | broadcast | bytes 147456 | tf_op jit(solution)/shard_map/broadcast_in_dim | solution.py:17
  17.5 5.1 %all-to-all-start.1 = ((bf16[8,64,128]{2,1,0:T(8,128)(2,1)}), bf16[8,64,128]{2,1,0:T(8,128)(2,1)S(1)}, u32[]{:S(2)}, u32[]{:S(2)}) async-start(bf16[8,64,128]{2,1,0:T(8,128)(2,1)} %broadcast_in_dim.10), calls=%async_computation.1 | async-start | bytes 262144 | tf_op jit(solution)/shard_map/all_to_all | solution.py:18
  22.6 0.5 %collective-permute-start.2 = (bf16[128,512]{1,0:T(8,128)(2,1)S(1)}, bf16[128,512]{1,0:T(8,128)(2,1)S(1)}, u32[]{:S(2)}, u32[]{:S(2)}) collective-permute-start(bf16[128,512]{1,0:T(8,128)(2,1)S(1)} %bitcast.81), channel_id=1, source_target_pairs={{0,16},{16,0},{1,17},{17,1},{2,18},{18,2},{3,19},{19,3},{4,20},{20... | collective-permute-start | bytes 393224 | tf_op jit(solution)/shard_map/ppermute | solution.py:41
  23.1 3.0 %all-to-all-done.1 = bf16[8,64,128]{2,1,0:T(8,128)(2,1)S(1)} async-done(((bf16[8,64,128]{2,1,0:T(8,128)(2,1)}), bf16[8,64,128]{2,1,0:T(8,128)(2,1)S(1)}, u32[]{:S(2)}, u32[]{:S(2)}) %all-to-all-start.1) | async-done | bytes 131104 | tf_op jit(solution)/shard_map/all_to_all | solution.py:18
  26.1 1.4 %collective-permute-done.2 = bf16[128,512]{1,0:T(8,128)(2,1)S(1)} collective-permute-done((bf16[128,512]{1,0:T(8,128)(2,1)S(1)}, bf16[128,512]{1,0:T(8,128)(2,1)S(1)}, u32[]{:S(2)}, u32[]{:S(2)}) %collective-permute-start.2) | collective-permute-done | bytes 131104 | tf_op jit(solution)/shard_map/ppermute | solution.py:41
  27.6 0.2 fusion
  27.8 0.1 slice_subtract_fusion.1
  27.9 0.1 fusion.6
  28.0 8.5 %all_to_all.15 = bf16[8,64,128]{2,1,0:T(8,128)(2,1)S(1)} all-to-all(bf16[8,64,128]{2,1,0:T(8,128)(2,1)S(1)} %broadcast_in_dim.11), channel_id=1, replica_groups={{10,8,6,4,2,0,14,12},{11,9,7,5,3,1,15,13},{26,24,22,20,18,16,30,28},{27..., dimensions={0} | all-to-all | bytes 262144 | tf_op jit(solution)/shard_map/all_to_all | solution.py:18
  36.5 0.2 fusion.11
  36.8 0.1 fusion.8
  36.9 0.7 %pad_maximum_fusion = bf16[1,64,128]{2,1,0:T(8,128)(2,1)} fusion(bf16[1,64,64]{2,1,0:T(8,128)(2,1)S(1)} %get-tuple-element.66, bf16[1,64,64]{2,1,0:T(8,128)(2,1)S(1)} %get-tuple-element.65), kind=kLoop, calls=%fused_computation.76 | loop fusion | flops 32768 | bytes 32768 | tf_op jit(solution)/shard_map/concatenate | solution.py:27
  (30 shorter events, 0.3 us)
Async XLA Ops:
  0.0 15.1 %collective-permute-start.1 = (bf16[64,128]{1,0:T(8,128)(2,1)}, bf16[64,128]{1,0:T(8,128)(2,1)S(1)}, u32[]{:S(2)}, u32[]{:S(2)}) collective-permute-start(bf16[64,128]{1,0:T(8,128)(2,1)} %bitcast.83), channel_id=1, source_target_pairs={{0,16},{16,0},{1,17},{17,1},{2,18},{18,2},{3,19},{19,3},{4,20},{20... | collective-permute-start | bytes 49160 | tf_op jit(solution)/shard_map/ppermute | solution.py:40
  4.4 7.0 %copy-start.2 = (bf16[1,2,64,512]{3,2,1,0:T(8,128)(2,1)S(1)}, bf16[1,2,64,512]{3,2,1,0:T(8,128)(2,1)}, u32[]{:S(2)}) copy-start(bf16[1,2,64,512]{3,2,1,0:T(8,128)(2,1)} %param.5) | copy-start | bytes 393220
  4.4 7.5 %copy-start.1 = (bf16[1,2,64,512]{3,2,1,0:T(8,128)(2,1)S(1)}, bf16[1,2,64,512]{3,2,1,0:T(8,128)(2,1)}, u32[]{:S(2)}) copy-start(bf16[1,2,64,512]{3,2,1,0:T(8,128)(2,1)} %param.7) | copy-start | bytes 393220
  4.4 10.7 %all-to-all-start = ((bf16[8,64,128]{2,1,0:T(8,128)(2,1)}), bf16[8,64,128]{2,1,0:T(8,128)(2,1)S(1)}, u32[]{:S(2)}, u32[]{:S(2)}) async-start(bf16[8,64,128]{2,1,0:T(8,128)(2,1)} %broadcast_in_dim.8), calls=%async_computation | async-start | bytes 262144 | tf_op jit(solution)/shard_map/all_to_all | solution.py:18
  11.4 5.0 %collective-permute-start = (bf16[128,512]{1,0:T(8,128)(2,1)S(1)}, bf16[128,512]{1,0:T(8,128)(2,1)S(1)}, u32[]{:S(2)}, u32[]{:S(2)}) collective-permute-start(bf16[128,512]{1,0:T(8,128)(2,1)S(1)} %bitcast.82), channel_id=1, source_target_pairs={{0,16},{16,0},{1,17},{17,1},{2,18},{18,2},{3,19},{19,3},{4,20},{20... | collective-permute-start | bytes 393224 | tf_op jit(solution)/shard_map/ppermute | solution.py:39
  11.9 0.7 %copy-start.3 = (bf16[1,64,128]{2,1,0:T(8,128)(2,1)S(1)}, bf16[1,64,128]{2,1,0:T(8,128)(2,1)}, u32[]{:S(2)}) copy-start(bf16[1,64,128]{2,1,0:T(8,128)(2,1)} %param.4) | copy-start | bytes 49156
  11.9 0.9 %copy-start = (bf16[1,2,64,512]{3,2,1,0:T(8,128)(2,1)S(1)}, bf16[1,2,64,512]{3,2,1,0:T(8,128)(2,1)}, u32[]{:S(2)}) copy-start(bf16[1,2,64,512]{3,2,1,0:T(8,128)(2,1)} %param.6) | copy-start | bytes 393220
  17.5 8.7 %all-to-all-start.1 = ((bf16[8,64,128]{2,1,0:T(8,128)(2,1)}), bf16[8,64,128]{2,1,0:T(8,128)(2,1)S(1)}, u32[]{:S(2)}, u32[]{:S(2)}) async-start(bf16[8,64,128]{2,1,0:T(8,128)(2,1)} %broadcast_in_dim.10), calls=%async_computation.1 | async-start | bytes 262144 | tf_op jit(solution)/shard_map/all_to_all | solution.py:18
  22.6 5.0 %collective-permute-start.2 = (bf16[128,512]{1,0:T(8,128)(2,1)S(1)}, bf16[128,512]{1,0:T(8,128)(2,1)S(1)}, u32[]{:S(2)}, u32[]{:S(2)}) collective-permute-start(bf16[128,512]{1,0:T(8,128)(2,1)S(1)} %bitcast.81), channel_id=1, source_target_pairs={{0,16},{16,0},{1,17},{17,1},{2,18},{18,2},{3,19},{19,3},{4,20},{20... | collective-permute-start | bytes 393224 | tf_op jit(solution)/shard_map/ppermute | solution.py:41

commit v3 on v1

v3 whole, which is shorter than its diff:
```python
import jax
import jax.numpy as jnp
from jax import lax
from jax.experimental import pallas as pl
from jax.experimental.pallas import tpu as pltpu
from jax.sharding import PartitionSpec as P


def from_behind(block, axis, distance):
    devices = range(lax.axis_size(axis))
    route = [(i - distance, i) for i in devices if i - distance in devices]
    return lax.ppermute(block, axis, route)


def group_order(devices):
    middle = devices // 2 + 1 if devices > 2 else 0
    return [(middle - i) % devices for i in range(devices)]


def exchange(copies):
    order = group_order(copies.shape[0])
    return lax.all_to_all(copies, "slab", split_axis=0, concat_axis=0, axis_index_groups=[order])


def gather_rows(rows):
    devices = lax.axis_size("slab")
    blocks = exchange(jnp.broadcast_to(rows[None], (devices,) + rows.shape))
    order = group_order(devices)
    return [blocks[order.index(i)] for i in range(devices)]


def complex_apply(matrix, blocks):
    vector = jnp.concatenate(blocks, axis=0)
    rows, half_cols = matrix.shape[0] // 2, vector.shape[1] // 2
    both = jnp.dot(matrix, vector, preferred_element_type=jnp.float32)
    real_part, imag_part = both[:rows], both[rows:]
    return jnp.concatenate(
        [
            real_part[:, :half_cols] - imag_part[:, half_cols:],
            real_part[:, half_cols:] + imag_part[:, :half_cols],
        ],
        axis=1,
    )


def in_order(blocks_ref):
    devices = blocks_ref.shape[0]
    order = group_order(devices)
    return [blocks_ref[order.index(i)] for i in range(devices)]


def hand_out(copies_ref, rows):
    for i in range(copies_ref.shape[0]):
        copies_ref[i] = rows


def prepare_kernel(src_ref, forward_ref, inverse_ref, upper_ref, bundle_ref, upper_out_ref, copies_ref, sems):
    height, order = forward_ref.shape
    rows = src_ref.shape[0]
    pairs = [
        (src_ref, bundle_ref.at[pl.ds(0, rows), pl.ds(2 * order, src_ref.shape[1])]),
        (src_ref, copies_ref.at[0]),
        (forward_ref, bundle_ref.at[:, pl.ds(0, order)]),
        (inverse_ref, bundle_ref.at[:, pl.ds(order, order)]),
        (upper_ref, upper_out_ref),
    ]
    copies = [pltpu.make_async_copy(a, b, sems.at[i]) for i, (a, b) in enumerate(pairs)]
    for copy in copies:
        copy.start()
    if height > rows:
        bundle_ref[rows:, 2 * order :] = jnp.zeros((height - rows, src_ref.shape[1]), bundle_ref.dtype)
    copies[0].wait()
    copies[1].wait()
    rows_in = copies_ref[0]
    for i in range(1, copies_ref.shape[0]):
        copies_ref[i] = rows_in
    for copy in copies[2:]:
        copy.wait()


def forward_kernel(other_ref, blocks_ref, copies_ref):
    order = blocks_ref.shape[0] * blocks_ref.shape[1]
    other_src = other_ref[: blocks_ref.shape[1], 2 * order :]
    first = lax.axis_index("sect") == 0

    @pl.when(first)
    def _():
        made = other_src.astype(jnp.float32) + complex_apply(other_ref[:, :order], in_order(blocks_ref))
        hand_out(copies_ref, made.astype(copies_ref.dtype))

    @pl.when(jnp.logical_not(first))
    def _():
        hand_out(copies_ref, other_src)


def wave_kernel(other_ref, bundle_ref, blocks_ref, copies_ref):
    order = blocks_ref.shape[0] * blocks_ref.shape[1]
    first = lax.axis_index("sect") == 0

    @pl.when(first)
    def _():
        made = complex_apply(other_ref[:, order : 2 * order], in_order(blocks_ref))
        hand_out(copies_ref, -made.astype(copies_ref.dtype))

    @pl.when(jnp.logical_not(first))
    def _():
        own_src = bundle_ref[: blocks_ref.shape[1], 2 * order :]
        made = own_src.astype(jnp.float32) + complex_apply(bundle_ref[:, :order], in_order(blocks_ref))
        hand_out(copies_ref, made.astype(copies_ref.dtype))


def last_kernel(bundle_ref, upper_ref, src_blocks_ref, blocks_ref, out_ref):
    order = blocks_ref.shape[0] * blocks_ref.shape[1]
    inverse = bundle_ref[:, order : 2 * order]
    first = lax.axis_index("sect") == 0

    @pl.when(first)
    def _():
        made = complex_apply(inverse, in_order(src_blocks_ref)) + complex_apply(upper_ref[...], in_order(blocks_ref))
        out_ref[...] = made.astype(out_ref.dtype)

    @pl.when(jnp.logical_not(first))
    def _():
        out_ref[...] = complex_apply(inverse, in_order(blocks_ref)).astype(out_ref.dtype)


def two_sections(src, forward, inverse, upper):
    devices = lax.axis_size("slab")
    height, order = forward.shape
    vmem = pl.BlockSpec(memory_space=pltpu.VMEM)
    small = pltpu.CompilerParams(vmem_limit_bytes=8 * 1024 * 1024)
    copies_shape = jax.ShapeDtypeStruct((devices,) + src.shape, src.dtype)
    bundle_shape = jax.ShapeDtypeStruct((height, 2 * order + src.shape[1]), src.dtype)
    bundle, upper, copies = pl.pallas_call(
        prepare_kernel,
        in_specs=[pl.BlockSpec(memory_space=pltpu.HBM)] * 4,
        out_specs=[vmem] * 3,
        out_shape=[bundle_shape, jax.ShapeDtypeStruct(upper.shape, upper.dtype), copies_shape],
        scratch_shapes=[pltpu.SemaphoreType.DMA((5,))],
        compiler_params=small, name="prepare",
    )(*(pltpu.with_memory_space_constraint(array, pltpu.HBM) for array in (src, forward, inverse, upper)))
    other = lax.ppermute(bundle, "sect", [(0, 1), (1, 0)])
    src_blocks = exchange(copies)
    other, src_blocks = lax.optimization_barrier((other, src_blocks))

    copies = pl.pallas_call(
        forward_kernel, in_specs=[vmem] * 2, out_specs=vmem, out_shape=copies_shape, compiler_params=small, name="forward"
    )(other, src_blocks)
    second = exchange(copies)
    copies = pl.pallas_call(
        wave_kernel, in_specs=[vmem] * 3, out_specs=vmem, out_shape=copies_shape, compiler_params=small, name="wave"
    )(other, bundle, second)
    third = exchange(copies)
    return pl.pallas_call(
        last_kernel, in_specs=[vmem] * 4, out_specs=vmem, out_shape=jax.ShapeDtypeStruct(src.shape, src.dtype), compiler_params=small, name="last"
    )(bundle, upper, src_blocks, third)


def many_sections(src, forward, inverse, upper):
    sections = lax.axis_size("sect")
    src_float = src.astype(jnp.float32)

    def forward_segment(segment_no, current):
        inflow = from_behind(current, "sect", 1)
        return (src_float + complex_apply(forward, gather_rows(inflow))).astype(jnp.bfloat16)

    forward_rows = lax.fori_loop(1, sections, forward_segment, src)
    scaled = complex_apply(inverse, gather_rows(forward_rows))

    def backward_segment(segment_no, current):
        outflow = from_behind(current, "sect", -1)
        return (scaled - complex_apply(upper, gather_rows(outflow))).astype(jnp.bfloat16)

    return lax.fori_loop(1, sections, backward_segment, scaled.astype(jnp.bfloat16))


def per_device(source, forward_mult, schur_inverse, upper_mult):
    src = source[0]
    forward, inverse, upper = (m[0].reshape(-1, m.shape[-1]) for m in (forward_mult, schur_inverse, upper_mult))
    run = two_sections if lax.axis_size("sect") == 2 else many_sections
    return run(src, forward, inverse, upper)[None]


def solution(mesh):
    in_specs = (
        P(("energy", "sect"), "slab", None),
        P(("energy", "sect"), None, "slab", None),
        P(("energy", "sect"), None, "slab", None),
        P(("energy", "sect"), None, "slab", None),
    )
    out_specs = P(("energy", "sect"), "slab", None)
    return jax.shard_map(
        per_device, mesh=mesh, in_specs=in_specs, out_specs=out_specs, check_vma=False
    )
```

time: 43.7 us -> 33.6 us (0.77)
  blocking collectives: 0 us -> 27.7 us
  waiting for transfers between devices: 21.6 us -> 0.01 us
  starting transfers between devices: 15.7 us -> 3.03 us
  local copies, waits for them, and re-layouts: 2.79 us -> 0 us
  Pallas kernels: 0 us -> 2.51 us
  other arithmetic: 2.2 us -> 0 us
  matrix products: 0.69 us -> 0 us
    all_to_all x0 -> x3, blocking collectives: none -> 27.7 us  [exchange(): lax.all_to_all(copies, 'slab', split_axis=0, concat_axis=0, axis_index_gr...]
    all_to_all x3 -> x0, waiting for transfers between devices: 21.6 us -> none  [gather_rows(): blocks = lax.all_to_all(copies, 'slab', split_axis=0, concat_axis=0)]
    all_to_all x3 -> x0, starting transfers between devices: 12.7 us -> none  [gather_rows(): blocks = lax.all_to_all(copies, 'slab', split_axis=0, concat_axis=0)]
    pallas_call x0 -> x4, Pallas kernels: none -> 2.51 us  [the longest x1 1.11 us: two_sections(): pl.pallas_call(prepare_kernel, in_specs=[pl.BlockSpec(memory_space=pltpu....]
    broadcast_in_dim x3 -> x0, local copies, waits for them, and re-layouts: 2.01 us -> none  [gather_rows(): copies = jnp.broadcast_to(rows[None], (devices,) + rows.shape)]
    concatenate x4 -> x0, other arithmetic: 1.24 us -> none  [the longest x1 0.99 us: two_sections(): bundle = jnp.concatenate([forward, inverse, flat], axis=0)]
    another operation x1 -> x0, local copies, waits for them, and re-layouts: 0.74 us -> none  [two_sections(): flat = src.reshape(-1, order)]
    convert_element_type x1 -> x0, other arithmetic: 0.7 us -> none  [two_sections(): return jnp.where(first, scaled - product, product).astype(jnp.bfloat16)]
  transfers between devices with their start and end apart: 4 -> 1, of which waited for: 3 -> 0; matrix products, arithmetic and copies ran while one was open for 2% -> 0% of each run, Pallas kernels for 0% -> 0%
where the time goes in v3:
time: 33.6 us; the launch traced here: 33.3 us
  blocking collectives  27.7 us (82%)
  starting transfers between devices  3.03 us (9%)
  Pallas kernels  2.51 us (7%)
    all_to_all x3, blocking collectives, exchange(): lax.all_to_all(copies, 'slab', split_axis=0, concat_axis=0, axis_index_gr...  27.7 us
    ppermute x1, starting transfers between devices, two_sections(): other = lax.ppermute(bundle, 'sect', [(0, 1), (1, 0)])  3.03 us
    pallas_call x1, Pallas kernels, two_sections(): pl.pallas_call(prepare_kernel, in_specs=[pl.BlockSpec(memory_space=pltpu....  1.11 us
    pallas_call x1, Pallas kernels, two_sections(): pl.pallas_call(last_kernel, in_specs=[vmem] * 4, out_specs=vmem, out_shap...  0.9 us
  transfers between devices with their start and end apart: 1, of which 0 were waited for; matrix products, arithmetic and copies ran while one was open for 0% of the time, Pallas kernels for 0%

profile of v3, /device:TPU:0, one launch (start us, length us, event | category | flops | bytes accessed | tf_op | source)
XLA Modules:
  0.0 33.3 jit_solution(3465042377746534416)
XLA Ops:
  0.0 1.1 %prepare.1 = (bf16[128,1152]{1,0:T(8,128)(2,1)S(1)}, bf16[128,512]{1,0:T(8,128)(2,1)S(1)}, bf16[8,64,128]{2,1,0:T(8,128)(2,1)S(1)}) custom-call(bf16[64,128]{1,0:T(8,128)(2,1)} %bitcast.8, bf16[128,512]{1,0:T(8,128)(2,1)} %bitcast.5, bf16[128,512]{1,0:T(8,128)(2,1)} %bitcast.6, bf16[128,512]{1,0:T(8,128)(2,1)} %bitcast.7), custom_call_target="tpu_custom_call" | custom-call | tf_op jit(solution)/shard_map/prepare/pallas_call | solution.py:134
  1.1 3.0 %collective-permute-start = (bf16[128,1152]{1,0:T(8,128)(2,1)S(1)}, bf16[128,1152]{1,0:T(8,128)(2,1)S(1)}, u32[]{:S(2)}, u32[]{:S(2)}) collective-permute-start(bf16[128,1152]{1,0:T(8,128)(2,1)S(1)} %get-tuple-element.10.bundle_ref), channel_id=1, source_target_pairs={{0,16},{16,0},{1,17},{17,1},{2,18},{18,2},{3,19},{19,3},{4,20},{20... | collective-permute-start | bytes 884744 | tf_op jit(solution)/shard_map/ppermute | solution.py:142
  4.1 9.7 %all_to_all.15.blocks_ref.src_blocks_ref = bf16[8,64,128]{2,1,0:T(8,128)(2,1)S(1)} all-to-all(bf16[8,64,128]{2,1,0:T(8,128)(2,1)S(1)} %get-tuple-element.12), channel_id=1, replica_groups={{10,8,6,4,2,0,14,12},{11,9,7,5,3,1,15,13},{26,24,22,20,18,16,30,28},{27..., dimensions={0} | all-to-all | bytes 262144 | tf_op jit(solution)/shard_map/all_to_all | solution.py:22
  13.9 0.0 collective-permute-done.other_ref
  13.9 0.3 forward.1
  14.2 9.0 %all_to_all.16.blocks_ref = bf16[8,64,128]{2,1,0:T(8,128)(2,1)S(1)} all-to-all(bf16[8,64,128]{2,1,0:T(8,128)(2,1)S(1)} %forward.1), channel_id=1, replica_groups={{10,8,6,4,2,0,14,12},{11,9,7,5,3,1,15,13},{26,24,22,20,18,16,30,28},{27..., dimensions={0} | all-to-all | bytes 262144 | tf_op jit(solution)/shard_map/all_to_all | solution.py:22
  23.1 0.3 wave.1
  23.4 9.0 %all_to_all.17.blocks_ref = bf16[8,64,128]{2,1,0:T(8,128)(2,1)S(1)} all-to-all(bf16[8,64,128]{2,1,0:T(8,128)(2,1)S(1)} %wave.1), channel_id=1, replica_groups={{10,8,6,4,2,0,14,12},{11,9,7,5,3,1,15,13},{26,24,22,20,18,16,30,28},{27..., dimensions={0} | all-to-all | bytes 262144 | tf_op jit(solution)/shard_map/all_to_all | solution.py:22
  32.4 0.9 %last.1 = bf16[64,128]{1,0:T(8,128)(2,1)} custom-call(bf16[128,1152]{1,0:T(8,128)(2,1)S(1)} %get-tuple-element.10.bundle_ref, bf16[128,512]{1,0:T(8,128)(2,1)S(1)} %get-tuple-element.11.upper_ref, bf16[8,64,128]{2,1,0:T(8,128)(2,1)S(1)} %all_to_all.15.blocks_ref.src_blocks_ref, bf16[8,64,128]{2,1,0:T(8,128)(2,1)S(1)} %all_to_all.17.blocks_ref), custom_call_target="tpu_custom_call" | custom-call | tf_op jit(solution)/shard_map/last/pallas_call | solution.py:154
Async XLA Ops:
  1.1 12.8 %collective-permute-start = (bf16[128,1152]{1,0:T(8,128)(2,1)S(1)}, bf16[128,1152]{1,0:T(8,128)(2,1)S(1)}, u32[]{:S(2)}, u32[]{:S(2)}) collective-permute-start(bf16[128,1152]{1,0:T(8,128)(2,1)S(1)} %get-tuple-element.10.bundle_ref), channel_id=1, source_target_pairs={{0,16},{16,0},{1,17},{17,1},{2,18},{18,2},{3,19},{19,3},{4,20},{20... | collective-permute-start | bytes 884744 | tf_op jit(solution)/shard_map/ppermute | solution.py:142

commit v4 on v3

v4 whole, which is shorter than its diff:
```python
import functools

import jax
import jax.numpy as jnp
from jax import lax
from jax.experimental import pallas as pl
from jax.experimental.pallas import tpu as pltpu
from jax.sharding import PartitionSpec as P


def from_behind(block, axis, distance):
    devices = range(lax.axis_size(axis))
    route = [(i - distance, i) for i in devices if i - distance in devices]
    return lax.ppermute(block, axis, route)


MEASURED = {8: (5, 1, 0, 2, 7, 3, 4, 6)}


def group_order(devices):
    middle = devices // 2 + 1 if devices > 2 else 0
    return list(MEASURED.get(devices, [(middle - i) % devices for i in range(devices)]))


def exchange(copies):
    order = group_order(copies.shape[0])
    return lax.all_to_all(copies, "slab", split_axis=0, concat_axis=0, axis_index_groups=[order])


def gather_rows(rows):
    devices = lax.axis_size("slab")
    blocks = exchange(jnp.broadcast_to(rows[None], (devices,) + rows.shape))
    order = group_order(devices)
    return [blocks[order.index(i)] for i in range(devices)]


def complex_apply(matrix, blocks):
    vector = jnp.concatenate(blocks, axis=0)
    rows, half_cols = matrix.shape[0] // 2, vector.shape[1] // 2
    both = jnp.dot(matrix, vector, preferred_element_type=jnp.float32)
    real_part, imag_part = both[:rows], both[rows:]
    return jnp.concatenate(
        [
            real_part[:, :half_cols] - imag_part[:, half_cols:],
            real_part[:, half_cols:] + imag_part[:, :half_cols],
        ],
        axis=1,
    )


def in_order(blocks_ref):
    devices = blocks_ref.shape[0]
    order = group_order(devices)
    return [blocks_ref[order.index(i)] for i in range(devices)]


def hand_out(copies_ref, rows):
    for i in range(copies_ref.shape[0]):
        copies_ref[i] = rows


def bundled(ref, height, src_shape):
    return ref.at[pl.ds(0, height)], ref.at[pl.ds(height, height)], ref.at[pl.ds(2 * height, src_shape[0]), pl.ds(0, src_shape[1])]


def prepare_kernel(src_ref, forward_ref, inverse_ref, upper_ref, bundle_ref, upper_out_ref, copies_ref, sems):
    forward_part, inverse_part, src_part = bundled(bundle_ref, forward_ref.shape[0], src_ref.shape)
    both = [(src_ref, src_part), (inverse_ref, inverse_part)]
    first_only = [(upper_ref, upper_out_ref)] + [(src_ref, copies_ref.at[i]) for i in range(copies_ref.shape[0])]
    second_only = [(forward_ref, forward_part)]

    def bring(pairs):
        moves = [pltpu.make_async_copy(a, b, sems.at[i]) for i, (a, b) in enumerate(pairs)]
        for move in moves:
            move.start()
        for move in moves:
            move.wait()

    first = lax.axis_index("sect") == 0

    @pl.when(first)
    def _():
        bring(first_only + both)

    @pl.when(jnp.logical_not(first))
    def _():
        bring(second_only + both)


def forward_kernel(height, other_ref, blocks_ref, copies_ref):
    other_forward, _, other_src = bundled(other_ref, height, blocks_ref.shape[1:])
    first = lax.axis_index("sect") == 0

    @pl.when(first)
    def _():
        made = other_src[...].astype(jnp.float32) + complex_apply(other_forward[...], in_order(blocks_ref))
        hand_out(copies_ref, made.astype(copies_ref.dtype))

    @pl.when(jnp.logical_not(first))
    def _():
        hand_out(copies_ref, other_src[...])


def wave_kernel(height, other_ref, bundle_ref, blocks_ref, copies_ref):
    _, other_inverse, _ = bundled(other_ref, height, blocks_ref.shape[1:])
    own_forward, _, own_src = bundled(bundle_ref, height, blocks_ref.shape[1:])
    first = lax.axis_index("sect") == 0

    @pl.when(first)
    def _():
        made = complex_apply(other_inverse[...], in_order(blocks_ref))
        hand_out(copies_ref, -made.astype(copies_ref.dtype))

    @pl.when(jnp.logical_not(first))
    def _():
        made = own_src[...].astype(jnp.float32) + complex_apply(own_forward[...], in_order(blocks_ref))
        hand_out(copies_ref, made.astype(copies_ref.dtype))


def last_kernel(height, bundle_ref, upper_ref, src_blocks_ref, blocks_ref, out_ref):
    _, inverse, _ = bundled(bundle_ref, height, blocks_ref.shape[1:])
    first = lax.axis_index("sect") == 0

    @pl.when(first)
    def _():
        made = complex_apply(inverse[...], in_order(src_blocks_ref)) + complex_apply(upper_ref[...], in_order(blocks_ref))
        out_ref[...] = made.astype(out_ref.dtype)

    @pl.when(jnp.logical_not(first))
    def _():
        out_ref[...] = complex_apply(inverse[...], in_order(blocks_ref)).astype(out_ref.dtype)


def two_sections(src, forward, inverse, upper):
    devices = lax.axis_size("slab")
    height, order = forward.shape
    vmem = pl.BlockSpec(memory_space=pltpu.VMEM)
    small = pltpu.CompilerParams(vmem_limit_bytes=8 * 1024 * 1024)
    copies_shape = jax.ShapeDtypeStruct((devices,) + src.shape, src.dtype)
    bundle_shape = jax.ShapeDtypeStruct((2 * height + src.shape[0], order), src.dtype)
    bundle, upper, copies = pl.pallas_call(
        prepare_kernel,
        in_specs=[pl.BlockSpec(memory_space=pltpu.HBM)] * 4,
        out_specs=[vmem] * 3,
        out_shape=[bundle_shape, jax.ShapeDtypeStruct(upper.shape, upper.dtype), copies_shape],
        scratch_shapes=[pltpu.SemaphoreType.DMA((devices + 3,))],
        compiler_params=small,
        name="prepare",
    )(*(pltpu.with_memory_space_constraint(array, pltpu.HBM) for array in (src, forward, inverse, upper)))
    other = lax.ppermute(bundle, "sect", [(0, 1), (1, 0)])
    src_blocks = exchange(copies)
    other, src_blocks = lax.optimization_barrier((other, src_blocks))

    def local(kernel, out_shape, *operands):
        return pl.pallas_call(
            functools.partial(kernel, height),
            in_specs=[vmem] * len(operands),
            out_specs=vmem,
            out_shape=out_shape,
            compiler_params=small,
        )(*operands)

    second = exchange(local(forward_kernel, copies_shape, other, src_blocks))
    third = exchange(local(wave_kernel, copies_shape, other, bundle, second))
    out_shape = jax.ShapeDtypeStruct(src.shape, src.dtype)
    return local(last_kernel, out_shape, bundle, upper, src_blocks, third)


def many_sections(src, forward, inverse, upper):
    sections = lax.axis_size("sect")
    src_float = src.astype(jnp.float32)

    def forward_segment(segment_no, current):
        inflow = from_behind(current, "sect", 1)
        return (src_float + complex_apply(forward, gather_rows(inflow))).astype(jnp.bfloat16)

    forward_rows = lax.fori_loop(1, sections, forward_segment, src)
    scaled = complex_apply(inverse, gather_rows(forward_rows))

    def backward_segment(segment_no, current):
        outflow = from_behind(current, "sect", -1)
        return (scaled - complex_apply(upper, gather_rows(outflow))).astype(jnp.bfloat16)

    return lax.fori_loop(1, sections, backward_segment, scaled.astype(jnp.bfloat16))


def per_device(source, forward_mult, schur_inverse, upper_mult):
    src = source[0]
    forward, inverse, upper = (m[0].reshape(-1, m.shape[-1]) for m in (forward_mult, schur_inverse, upper_mult))
    run = two_sections if lax.axis_size("sect") == 2 else many_sections
    return run(src, forward, inverse, upper)[None]


def solution(mesh):
    in_specs = (
        P(("energy", "sect"), "slab", None),
        P(("energy", "sect"), None, "slab", None),
        P(("energy", "sect"), None, "slab", None),
        P(("energy", "sect"), None, "slab", None),
    )
    out_specs = P(("energy", "sect"), "slab", None)
    return jax.shard_map(
        per_device, mesh=mesh, in_specs=in_specs, out_specs=out_specs, check_vma=False
    )
```

time: 33.6 us -> 33.1 us (0.985)
  blocking collectives: 27.7 us -> 27.3 us
    all_to_all x3, blocking collectives: 27.7 us -> 27.3 us  [exchange(): lax.all_to_all(copies, 'slab', split_axis=0, concat_axis=0, axis_index_gr...]
where the time goes in v4:
time: 33.1 us; the launch traced here: 32.9 us
  blocking collectives  27.3 us (82%)
  starting transfers between devices  2.92 us (9%)
  Pallas kernels  2.59 us (8%)
    all_to_all x3, blocking collectives, exchange(): lax.all_to_all(copies, 'slab', split_axis=0, concat_axis=0, axis_index_gr...  27.3 us
    ppermute x1, starting transfers between devices, two_sections(): other = lax.ppermute(bundle, 'sect', [(0, 1), (1, 0)])  2.92 us
    pallas_call x3, Pallas kernels, local(): pl.pallas_call(functools.partial(kernel, height), in_specs=[vmem] * len(o...  1.4 us
    pallas_call x1, Pallas kernels, two_sections(): pl.pallas_call(prepare_kernel, in_specs=[pl.BlockSpec(memory_space=pltpu....  1.19 us
  transfers between devices with their start and end apart: 1, of which 0 were waited for; matrix products, arithmetic and copies ran while one was open for 0% of the time, Pallas kernels for 0%

profile of v4, /device:TPU:0, one launch (start us, length us, event | category | flops | bytes accessed | tf_op | source)
XLA Modules:
  0.0 32.9 jit_solution(6719749757750267041)
XLA Ops:
  0.0 1.2 %prepare.1 = (bf16[320,512]{1,0:T(8,128)(2,1)S(1)}, bf16[128,512]{1,0:T(8,128)(2,1)S(1)}, bf16[8,64,128]{2,1,0:T(8,128)(2,1)S(1)}) custom-call(bf16[64,128]{1,0:T(8,128)(2,1)} %bitcast.8, bf16[128,512]{1,0:T(8,128)(2,1)} %bitcast.5, bf16[128,512]{1,0:T(8,128)(2,1)} %bitcast.6, bf16[128,512]{1,0:T(8,128)(2,1)} %bitcast.7), custom_call_target="tpu_custom_call" | custom-call | tf_op jit(solution)/shard_map/prepare/pallas_call | solution.py:141
  1.2 2.9 %collective-permute-start = (bf16[320,512]{1,0:T(8,128)(2,1)S(1)}, bf16[320,512]{1,0:T(8,128)(2,1)S(1)}, u32[]{:S(2)}, u32[]{:S(2)}) collective-permute-start(bf16[320,512]{1,0:T(8,128)(2,1)S(1)} %get-tuple-element.10.bundle_ref), channel_id=1, source_target_pairs={{0,16},{16,0},{1,17},{17,1},{2,18},{18,2},{3,19},{19,3},{4,20},{20... | collective-permute-start | bytes 983048 | tf_op jit(solution)/shard_map/ppermute | solution.py:150
  4.1 9.7 %all_to_all.15.blocks_ref.src_blocks_ref = bf16[8,64,128]{2,1,0:T(8,128)(2,1)S(1)} all-to-all(bf16[8,64,128]{2,1,0:T(8,128)(2,1)S(1)} %get-tuple-element.12), channel_id=1, replica_groups={{10,2,0,4,14,6,8,12},{11,3,1,5,15,7,9,13},{26,18,16,20,30,22,24,28},{27..., dimensions={0} | all-to-all | bytes 262144 | tf_op jit(solution)/shard_map/all_to_all | solution.py:27
  13.9 0.0 collective-permute-done.other_ref
  13.9 0.3 shard_map.46
  14.1 8.8 %all_to_all.16.blocks_ref = bf16[8,64,128]{2,1,0:T(8,128)(2,1)S(1)} all-to-all(bf16[8,64,128]{2,1,0:T(8,128)(2,1)S(1)} %shard_map.46), channel_id=1, replica_groups={{10,2,0,4,14,6,8,12},{11,3,1,5,15,7,9,13},{26,18,16,20,30,22,24,28},{27..., dimensions={0} | all-to-all | bytes 262144 | tf_op jit(solution)/shard_map/all_to_all | solution.py:27
  22.9 0.3 shard_map.47
  23.2 8.8 %all_to_all.17.blocks_ref = bf16[8,64,128]{2,1,0:T(8,128)(2,1)S(1)} all-to-all(bf16[8,64,128]{2,1,0:T(8,128)(2,1)S(1)} %shard_map.47), channel_id=1, replica_groups={{10,2,0,4,14,6,8,12},{11,3,1,5,15,7,9,13},{26,18,16,20,30,22,24,28},{27..., dimensions={0} | all-to-all | bytes 262144 | tf_op jit(solution)/shard_map/all_to_all | solution.py:27
  32.0 0.9 %shard_map.48 = bf16[64,128]{1,0:T(8,128)(2,1)} custom-call(bf16[320,512]{1,0:T(8,128)(2,1)S(1)} %get-tuple-element.10.bundle_ref, bf16[128,512]{1,0:T(8,128)(2,1)S(1)} %get-tuple-element.11.upper_ref, bf16[8,64,128]{2,1,0:T(8,128)(2,1)S(1)} %all_to_all.15.blocks_ref.src_blocks_ref, bf16[8,64,128]{2,1,0:T(8,128)(2,1)S(1)} %all_to_all.17.blocks_ref), custom_call_target="tpu_custom_call" | custom-call | tf_op jit(solution)/shard_map/pallas_call | solution.py:155
Async XLA Ops:
  1.2 12.7 %collective-permute-start = (bf16[320,512]{1,0:T(8,128)(2,1)S(1)}, bf16[320,512]{1,0:T(8,128)(2,1)S(1)}, u32[]{:S(2)}, u32[]{:S(2)}) collective-permute-start(bf16[320,512]{1,0:T(8,128)(2,1)S(1)} %get-tuple-element.10.bundle_ref), channel_id=1, source_target_pairs={{0,16},{16,0},{1,17},{17,1},{2,18},{18,2},{3,19},{19,3},{4,20},{20... | collective-permute-start | bytes 983048 | tf_op jit(solution)/shard_map/ppermute | solution.py:150

commit v5 on v4

--- a/solution.py
+++ b/solution.py
@@ -34,10 +34,8 @@
     return [blocks[order.index(i)] for i in range(devices)]
 
 
-def complex_apply(matrix, blocks):
-    vector = jnp.concatenate(blocks, axis=0)
-    rows, half_cols = matrix.shape[0] // 2, vector.shape[1] // 2
-    both = jnp.dot(matrix, vector, preferred_element_type=jnp.float32)
+def combined(both):
+    rows, half_cols = both.shape[0] // 2, both.shape[1] // 2
     real_part, imag_part = both[:rows], both[rows:]
     return jnp.concatenate(
         [
@@ -48,6 +46,14 @@
     )
 
 
+def product(matrix, blocks):
+    return jnp.dot(matrix, jnp.concatenate(blocks, axis=0), preferred_element_type=jnp.float32)
+
+
+def complex_apply(matrix, blocks):
+    return combined(product(matrix, blocks))
+
+
 def in_order(blocks_ref):
     devices = blocks_ref.shape[0]
     order = group_order(devices)
@@ -63,28 +69,38 @@
     return ref.at[pl.ds(0, height)], ref.at[pl.ds(height, height)], ref.at[pl.ds(2 * height, src_shape[0]), pl.ds(0, src_shape[1])]
 
 
+def pieces(from_ref, to_ref):
+    rows = from_ref.shape[0] // 2
+    return [(from_ref.at[pl.ds(i * rows, rows)], to_ref.at[pl.ds(i * rows, rows)]) for i in range(2)]
+
+
 def prepare_kernel(src_ref, forward_ref, inverse_ref, upper_ref, bundle_ref, upper_out_ref, copies_ref, sems):
     forward_part, inverse_part, src_part = bundled(bundle_ref, forward_ref.shape[0], src_ref.shape)
-    both = [(src_ref, src_part), (inverse_ref, inverse_part)]
-    first_only = [(upper_ref, upper_out_ref)] + [(src_ref, copies_ref.at[i]) for i in range(copies_ref.shape[0])]
-    second_only = [(forward_ref, forward_part)]
 
     def bring(pairs):
         moves = [pltpu.make_async_copy(a, b, sems.at[i]) for i, (a, b) in enumerate(pairs)]
         for move in moves:
             move.start()
-        for move in moves:
+        return moves
+
+    first = lax.axis_index("sect") == 0
+
+    @pl.when(first)
+    def _():
+        moves = bring([(src_ref, copies_ref.at[0]), (inverse_ref, inverse_part), (upper_ref, upper_out_ref)])
+        moves[0].wait()
+        rows = copies_ref[0]
+        src_part[...] = rows
+        for i in range(1, copies_ref.shape[0]):
+            copies_ref[i] = rows
+        for move in moves[1:]:
             move.wait()
 
-    first = lax.axis_index("sect") == 0
-
-    @pl.when(first)
-    def _():
-        bring(first_only + both)
-
-    @pl.when(jnp.logical_not(first))
-    def _():
-        bring(second_only + both)
+    @pl.when(jnp.logical_not(first))
+    def _():
+        halves = pieces(forward_ref, forward_part) + pieces(inverse_ref, inverse_part)
+        for move in bring(halves + [(src_ref, src_part)]):
+            move.wait()
 
 
 def forward_kernel(height, other_ref, blocks_ref, copies_ref):
@@ -123,8 +139,8 @@
 
     @pl.when(first)
     def _():
-        made = complex_apply(inverse[...], in_order(src_blocks_ref)) + complex_apply(upper_ref[...], in_order(blocks_ref))
-        out_ref[...] = made.astype(out_ref.dtype)
+        both = product(inverse[...], in_order(src_blocks_ref)) + product(upper_ref[...], in_order(blocks_ref))
+        out_ref[...] = combined(both).astype(out_ref.dtype)
 
     @pl.when(jnp.logical_not(first))
     def _():
@@ -143,7 +159,7 @@
         in_specs=[pl.BlockSpec(memory_space=pltpu.HBM)] * 4,
         out_specs=[vmem] * 3,
         out_shape=[bundle_shape, jax.ShapeDtypeStruct(upper.shape, upper.dtype), copies_shape],
-        scratch_shapes=[pltpu.SemaphoreType.DMA((devices + 3,))],
+        scratch_shapes=[pltpu.SemaphoreType.DMA((5,))],
         compiler_params=small,
         name="prepare",
     )(*(pltpu.with_memory_space_constraint(array, pltpu.HBM) for array in (src, forward, inverse, upper)))

time: 33.1 us -> 33.1 us (level)
  no operation moved by 1% of the time
where the time goes in v5:
time: 33.1 us; the launch traced here: 32.8 us
  blocking collectives  27.4 us (83%)
  starting transfers between devices  2.98 us (9%)
  Pallas kernels  2.42 us (7%)
    all_to_all x3, blocking collectives, exchange(): lax.all_to_all(copies, 'slab', split_axis=0, concat_axis=0, axis_index_gr...  27.4 us
    ppermute x1, starting transfers between devices, two_sections(): other = lax.ppermute(bundle, 'sect', [(0, 1), (1, 0)])  2.98 us
    pallas_call x3, Pallas kernels, local(): pl.pallas_call(functools.partial(kernel, height), in_specs=[vmem] * len(o...  1.4 us
    pallas_call x1, Pallas kernels, two_sections(): pl.pallas_call(prepare_kernel, in_specs=[pl.BlockSpec(memory_space=pltpu....  1.03 us
  transfers between devices with their start and end apart: 1, of which 0 were waited for; matrix products, arithmetic and copies ran while one was open for 0% of the time, Pallas kernels for 0%

profile of v5, /device:TPU:0, one launch (start us, length us, event | category | flops | bytes accessed | tf_op | source)
XLA Modules:
  0.0 32.8 jit_solution(11226935059761294832)
XLA Ops:
  0.0 1.0 %prepare.1 = (bf16[320,512]{1,0:T(8,128)(2,1)S(1)}, bf16[128,512]{1,0:T(8,128)(2,1)S(1)}, bf16[8,64,128]{2,1,0:T(8,128)(2,1)S(1)}) custom-call(bf16[64,128]{1,0:T(8,128)(2,1)} %bitcast.8, bf16[128,512]{1,0:T(8,128)(2,1)} %bitcast.5, bf16[128,512]{1,0:T(8,128)(2,1)} %bitcast.6, bf16[128,512]{1,0:T(8,128)(2,1)} %bitcast.7), custom_call_target="tpu_custom_call" | custom-call | tf_op jit(solution)/shard_map/prepare/pallas_call | solution.py:157
  1.0 3.0 %collective-permute-start = (bf16[320,512]{1,0:T(8,128)(2,1)S(1)}, bf16[320,512]{1,0:T(8,128)(2,1)S(1)}, u32[]{:S(2)}, u32[]{:S(2)}) collective-permute-start(bf16[320,512]{1,0:T(8,128)(2,1)S(1)} %get-tuple-element.10.bundle_ref), channel_id=1, source_target_pairs={{0,16},{16,0},{1,17},{17,1},{2,18},{18,2},{3,19},{19,3},{4,20},{20... | collective-permute-start | bytes 983048 | tf_op jit(solution)/shard_map/ppermute | solution.py:166
  4.0 9.7 %all_to_all.15.blocks_ref.src_blocks_ref = bf16[8,64,128]{2,1,0:T(8,128)(2,1)S(1)} all-to-all(bf16[8,64,128]{2,1,0:T(8,128)(2,1)S(1)} %get-tuple-element.12), channel_id=1, replica_groups={{10,2,0,4,14,6,8,12},{11,3,1,5,15,7,9,13},{26,18,16,20,30,22,24,28},{27..., dimensions={0} | all-to-all | bytes 262144 | tf_op jit(solution)/shard_map/all_to_all | solution.py:27
  13.8 0.0 collective-permute-done.other_ref
  13.8 0.2 shard_map.46
  14.0 8.8 %all_to_all.16.blocks_ref = bf16[8,64,128]{2,1,0:T(8,128)(2,1)S(1)} all-to-all(bf16[8,64,128]{2,1,0:T(8,128)(2,1)S(1)} %shard_map.46), channel_id=1, replica_groups={{10,2,0,4,14,6,8,12},{11,3,1,5,15,7,9,13},{26,18,16,20,30,22,24,28},{27..., dimensions={0} | all-to-all | bytes 262144 | tf_op jit(solution)/shard_map/all_to_all | solution.py:27
  22.8 0.3 shard_map.47
  23.1 8.8 %all_to_all.17.blocks_ref = bf16[8,64,128]{2,1,0:T(8,128)(2,1)S(1)} all-to-all(bf16[8,64,128]{2,1,0:T(8,128)(2,1)S(1)} %shard_map.47), channel_id=1, replica_groups={{10,2,0,4,14,6,8,12},{11,3,1,5,15,7,9,13},{26,18,16,20,30,22,24,28},{27..., dimensions={0} | all-to-all | bytes 262144 | tf_op jit(solution)/shard_map/all_to_all | solution.py:27
  31.9 0.9 %shard_map.48 = bf16[64,128]{1,0:T(8,128)(2,1)} custom-call(bf16[320,512]{1,0:T(8,128)(2,1)S(1)} %get-tuple-element.10.bundle_ref, bf16[128,512]{1,0:T(8,128)(2,1)S(1)} %get-tuple-element.11.upper_ref, bf16[8,64,128]{2,1,0:T(8,128)(2,1)S(1)} %all_to_all.15.blocks_ref.src_blocks_ref, bf16[8,64,128]{2,1,0:T(8,128)(2,1)S(1)} %all_to_all.17.blocks_ref), custom_call_target="tpu_custom_call" | custom-call | tf_op jit(solution)/shard_map/pallas_call | solution.py:171
Async XLA Ops:
  1.0 12.7 %collective-permute-start = (bf16[320,512]{1,0:T(8,128)(2,1)S(1)}, bf16[320,512]{1,0:T(8,128)(2,1)S(1)}, u32[]{:S(2)}, u32[]{:S(2)}) collective-permute-start(bf16[320,512]{1,0:T(8,128)(2,1)S(1)} %get-tuple-element.10.bundle_ref), channel_id=1, source_target_pairs={{0,16},{16,0},{1,17},{17,1},{2,18},{18,2},{3,19},{19,3},{4,20},{20... | collective-permute-start | bytes 983048 | tf_op jit(solution)/shard_map/ppermute | solution.py:166

commit v6 on v5

--- a/solution.py
+++ b/solution.py
@@ -32,6 +32,10 @@
     blocks = exchange(jnp.broadcast_to(rows[None], (devices,) + rows.shape))
     order = group_order(devices)
     return [blocks[order.index(i)] for i in range(devices)]
+
+
+def complex_apply(matrix, blocks):
+    return combined(jnp.dot(matrix, jnp.concatenate(blocks, axis=0), preferred_element_type=jnp.float32))
 
 
 def combined(both):
@@ -46,14 +50,6 @@
     )
 
 
-def product(matrix, blocks):
-    return jnp.dot(matrix, jnp.concatenate(blocks, axis=0), preferred_element_type=jnp.float32)
-
-
-def complex_apply(matrix, blocks):
-    return combined(product(matrix, blocks))
-
-
 def in_order(blocks_ref):
     devices = blocks_ref.shape[0]
     order = group_order(devices)
@@ -67,11 +63,6 @@
 
 def bundled(ref, height, src_shape):
     return ref.at[pl.ds(0, height)], ref.at[pl.ds(height, height)], ref.at[pl.ds(2 * height, src_shape[0]), pl.ds(0, src_shape[1])]
-
-
-def pieces(from_ref, to_ref):
-    rows = from_ref.shape[0] // 2
-    return [(from_ref.at[pl.ds(i * rows, rows)], to_ref.at[pl.ds(i * rows, rows)]) for i in range(2)]
 
 
 def prepare_kernel(src_ref, forward_ref, inverse_ref, upper_ref, bundle_ref, upper_out_ref, copies_ref, sems):
@@ -98,19 +89,22 @@
 
     @pl.when(jnp.logical_not(first))
     def _():
-        halves = pieces(forward_ref, forward_part) + pieces(inverse_ref, inverse_part)
-        for move in bring(halves + [(src_ref, src_part)]):
+        for move in bring([(forward_ref, forward_part), (inverse_ref, inverse_part), (src_ref, src_part)]):
             move.wait()
 
 
-def forward_kernel(height, other_ref, blocks_ref, copies_ref):
+def forward_kernel(height, other_ref, bundle_ref, blocks_ref, copies_ref, scaled_ref):
     other_forward, _, other_src = bundled(other_ref, height, blocks_ref.shape[1:])
-    first = lax.axis_index("sect") == 0
-
-    @pl.when(first)
-    def _():
-        made = other_src[...].astype(jnp.float32) + complex_apply(other_forward[...], in_order(blocks_ref))
+    _, inverse, _ = bundled(bundle_ref, height, blocks_ref.shape[1:])
+    first = lax.axis_index("sect") == 0
+
+    @pl.when(first)
+    def _():
+        stacked = jnp.concatenate([other_forward[...], inverse[...]], axis=0)
+        both = jnp.dot(stacked, jnp.concatenate(in_order(blocks_ref), axis=0), preferred_element_type=jnp.float32)
+        made = other_src[...].astype(jnp.float32) + combined(both[:height])
         hand_out(copies_ref, made.astype(copies_ref.dtype))
+        scaled_ref[...] = combined(both[height:])
 
     @pl.when(jnp.logical_not(first))
     def _():
@@ -133,14 +127,14 @@
         hand_out(copies_ref, made.astype(copies_ref.dtype))
 
 
-def last_kernel(height, bundle_ref, upper_ref, src_blocks_ref, blocks_ref, out_ref):
+def last_kernel(height, bundle_ref, upper_ref, scaled_ref, blocks_ref, out_ref):
     _, inverse, _ = bundled(bundle_ref, height, blocks_ref.shape[1:])
     first = lax.axis_index("sect") == 0
 
     @pl.when(first)
     def _():
-        both = product(inverse[...], in_order(src_blocks_ref)) + product(upper_ref[...], in_order(blocks_ref))
-        out_ref[...] = combined(both).astype(out_ref.dtype)
+        made = scaled_ref[...] + complex_apply(upper_ref[...], in_order(blocks_ref))
+        out_ref[...] = made.astype(out_ref.dtype)
 
     @pl.when(jnp.logical_not(first))
     def _():
@@ -159,7 +153,7 @@
         in_specs=[pl.BlockSpec(memory_space=pltpu.HBM)] * 4,
         out_specs=[vmem] * 3,
         out_shape=[bundle_shape, jax.ShapeDtypeStruct(upper.shape, upper.dtype), copies_shape],
-        scratch_shapes=[pltpu.SemaphoreType.DMA((5,))],
+        scratch_shapes=[pltpu.SemaphoreType.DMA((3,))],
         compiler_params=small,
         name="prepare",
     )(*(pltpu.with_memory_space_constraint(array, pltpu.HBM) for array in (src, forward, inverse, upper)))
@@ -171,15 +165,17 @@
         return pl.pallas_call(
             functools.partial(kernel, height),
             in_specs=[vmem] * len(operands),
-            out_specs=vmem,
+            out_specs=jax.tree.map(lambda _: vmem, out_shape),
             out_shape=out_shape,
             compiler_params=small,
         )(*operands)
 
-    second = exchange(local(forward_kernel, copies_shape, other, src_blocks))
+    scaled_shape = jax.ShapeDtypeStruct(src.shape, jnp.float32)
+    copies, scaled = local(forward_kernel, (copies_shape, scaled_shape), other, bundle, src_blocks)
+    second = exchange(copies)
     third = exchange(local(wave_kernel, copies_shape, other, bundle, second))
     out_shape = jax.ShapeDtypeStruct(src.shape, src.dtype)
-    return local(last_kernel, out_shape, bundle, upper, src_blocks, third)
+    return local(last_kernel, out_shape, bundle, upper, scaled, third)
 
 
 def many_sections(src, forward, inverse, upper):

time: 33.1 us -> 33.1 us (level)
  no operation moved by 1% of the time
where the time goes in v6:
time: 33.1 us; the launch traced here: 32.8 us
  blocking collectives  27.4 us (83%)
  starting transfers between devices  3.02 us (9%)
  Pallas kernels  2.39 us (7%)
    all_to_all x3, blocking collectives, exchange(): lax.all_to_all(copies, 'slab', split_axis=0, concat_axis=0, axis_index_gr...  27.4 us
    ppermute x1, starting transfers between devices, two_sections(): other = lax.ppermute(bundle, 'sect', [(0, 1), (1, 0)])  3.02 us
    pallas_call x3, Pallas kernels, local(): pl.pallas_call(functools.partial(kernel, height), in_specs=[vmem] * len(o...  1.39 us
    pallas_call x1, Pallas kernels, two_sections(): pl.pallas_call(prepare_kernel, in_specs=[pl.BlockSpec(memory_space=pltpu....  1.01 us
  transfers between devices with their start and end apart: 1, of which 0 were waited for; matrix products, arithmetic and copies ran while one was open for 0% of the time, Pallas kernels for 0%

profile of v6, /device:TPU:0, one launch (start us, length us, event | category | flops | bytes accessed | tf_op | source)
XLA Modules:
  0.0 32.8 jit_solution(4923127307000637969)
XLA Ops:
  0.0 1.0 %prepare.1 = (bf16[320,512]{1,0:T(8,128)(2,1)S(1)}, bf16[128,512]{1,0:T(8,128)(2,1)S(1)}, bf16[8,64,128]{2,1,0:T(8,128)(2,1)S(1)}) custom-call(bf16[64,128]{1,0:T(8,128)(2,1)} %bitcast.8, bf16[128,512]{1,0:T(8,128)(2,1)} %bitcast.5, bf16[128,512]{1,0:T(8,128)(2,1)} %bitcast.6, bf16[128,512]{1,0:T(8,128)(2,1)} %bitcast.7), custom_call_target="tpu_custom_call" | custom-call | tf_op jit(solution)/shard_map/prepare/pallas_call | solution.py:151
  1.0 3.0 %collective-permute-start = (bf16[320,512]{1,0:T(8,128)(2,1)S(1)}, bf16[320,512]{1,0:T(8,128)(2,1)S(1)}, u32[]{:S(2)}, u32[]{:S(2)}) collective-permute-start(bf16[320,512]{1,0:T(8,128)(2,1)S(1)} %get-tuple-element.12.bundle_ref), channel_id=1, source_target_pairs={{0,16},{16,0},{1,17},{17,1},{2,18},{18,2},{3,19},{19,3},{4,20},{20... | collective-permute-start | bytes 983048 | tf_op jit(solution)/shard_map/ppermute | solution.py:160
  4.0 9.7 %all_to_all.15.blocks_ref = bf16[8,64,128]{2,1,0:T(8,128)(2,1)S(1)} all-to-all(bf16[8,64,128]{2,1,0:T(8,128)(2,1)S(1)} %get-tuple-element.14), channel_id=1, replica_groups={{10,2,0,4,14,6,8,12},{11,3,1,5,15,7,9,13},{26,18,16,20,30,22,24,28},{27..., dimensions={0} | all-to-all | bytes 262144 | tf_op jit(solution)/shard_map/all_to_all | solution.py:27
  13.8 0.0 collective-permute-done.other_ref
  13.8 0.3 shard_map.46
  14.1 8.8 %all_to_all.16.blocks_ref = bf16[8,64,128]{2,1,0:T(8,128)(2,1)S(1)} all-to-all(bf16[8,64,128]{2,1,0:T(8,128)(2,1)S(1)} %get-tuple-element.18), channel_id=1, replica_groups={{10,2,0,4,14,6,8,12},{11,3,1,5,15,7,9,13},{26,18,16,20,30,22,24,28},{27..., dimensions={0} | all-to-all | bytes 262144 | tf_op jit(solution)/shard_map/all_to_all | solution.py:27
  22.9 0.3 shard_map.47
  23.1 8.8 %all_to_all.17.blocks_ref = bf16[8,64,128]{2,1,0:T(8,128)(2,1)S(1)} all-to-all(bf16[8,64,128]{2,1,0:T(8,128)(2,1)S(1)} %shard_map.47), channel_id=1, replica_groups={{10,2,0,4,14,6,8,12},{11,3,1,5,15,7,9,13},{26,18,16,20,30,22,24,28},{27..., dimensions={0} | all-to-all | bytes 262144 | tf_op jit(solution)/shard_map/all_to_all | solution.py:27
  31.9 0.9 %shard_map.48 = bf16[64,128]{1,0:T(8,128)(2,1)} custom-call(bf16[320,512]{1,0:T(8,128)(2,1)S(1)} %get-tuple-element.12.bundle_ref, bf16[128,512]{1,0:T(8,128)(2,1)S(1)} %get-tuple-element.13.upper_ref, f32[64,128]{1,0:T(8,128)S(1)} %get-tuple-element.17.scaled_ref, bf16[8,64,128]{2,1,0:T(8,128)(2,1)S(1)} %all_to_all.17.blocks_ref), custom_call_target="tpu_custom_call" | custom-call | tf_op jit(solution)/shard_map/pallas_call | solution.py:165
Async XLA Ops:
  1.0 12.8 %collective-permute-start = (bf16[320,512]{1,0:T(8,128)(2,1)S(1)}, bf16[320,512]{1,0:T(8,128)(2,1)S(1)}, u32[]{:S(2)}, u32[]{:S(2)}) collective-permute-start(bf16[320,512]{1,0:T(8,128)(2,1)S(1)} %get-tuple-element.12.bundle_ref), channel_id=1, source_target_pairs={{0,16},{16,0},{1,17},{17,1},{2,18},{18,2},{3,19},{19,3},{4,20},{20... | collective-permute-start | bytes 983048 | tf_op jit(solution)/shard_map/ppermute | solution.py:160

commit v7 on v6

--- a/solution.py
+++ b/solution.py
@@ -65,6 +65,11 @@
     return ref.at[pl.ds(0, height)], ref.at[pl.ds(height, height)], ref.at[pl.ds(2 * height, src_shape[0]), pl.ds(0, src_shape[1])]
 
 
+def pieces(from_ref, to_ref):
+    rows = from_ref.shape[0] // 2
+    return [(from_ref.at[pl.ds(i * rows, rows)], to_ref.at[pl.ds(i * rows, rows)]) for i in range(2)]
+
+
 def prepare_kernel(src_ref, forward_ref, inverse_ref, upper_ref, bundle_ref, upper_out_ref, copies_ref, sems):
     forward_part, inverse_part, src_part = bundled(bundle_ref, forward_ref.shape[0], src_ref.shape)
 
@@ -89,7 +94,8 @@
 
     @pl.when(jnp.logical_not(first))
     def _():
-        for move in bring([(forward_ref, forward_part), (inverse_ref, inverse_part), (src_ref, src_part)]):
+        halves = pieces(forward_ref, forward_part) + pieces(inverse_ref, inverse_part)
+        for move in bring(halves + [(src_ref, src_part)]):
             move.wait()
 
 
@@ -153,7 +159,7 @@
         in_specs=[pl.BlockSpec(memory_space=pltpu.HBM)] * 4,
         out_specs=[vmem] * 3,
         out_shape=[bundle_shape, jax.ShapeDtypeStruct(upper.shape, upper.dtype), copies_shape],
-        scratch_shapes=[pltpu.SemaphoreType.DMA((3,))],
+        scratch_shapes=[pltpu.SemaphoreType.DMA((5,))],
         compiler_params=small,
         name="prepare",
     )(*(pltpu.with_memory_space_constraint(array, pltpu.HBM) for array in (src, forward, inverse, upper)))

time: 33.1 us -> 33.1 us (level)
  no operation moved by 1% of the time
where the time goes in v7:
time: 33.1 us; the launch traced here: 32.8 us
  blocking collectives  27.4 us (83%)
  starting transfers between devices  2.98 us (9%)
  Pallas kernels  2.41 us (7%)
    all_to_all x3, blocking collectives, exchange(): lax.all_to_all(copies, 'slab', split_axis=0, concat_axis=0, axis_index_gr...  27.4 us
    ppermute x1, starting transfers between devices, two_sections(): other = lax.ppermute(bundle, 'sect', [(0, 1), (1, 0)])  2.98 us
    pallas_call x3, Pallas kernels, local(): pl.pallas_call(functools.partial(kernel, height), in_specs=[vmem] * len(o...  1.39 us
    pallas_call x1, Pallas kernels, two_sections(): pl.pallas_call(prepare_kernel, in_specs=[pl.BlockSpec(memory_space=pltpu....  1.03 us
  transfers between devices with their start and end apart: 1, of which 0 were waited for; matrix products, arithmetic and copies ran while one was open for 0% of the time, Pallas kernels for 0%

profile of v7, /device:TPU:0, one launch (start us, length us, event | category | flops | bytes accessed | tf_op | source)
XLA Modules:
  0.0 32.8 jit_solution(4953265591103217034)
XLA Ops:
  0.0 1.0 %prepare.1 = (bf16[320,512]{1,0:T(8,128)(2,1)S(1)}, bf16[128,512]{1,0:T(8,128)(2,1)S(1)}, bf16[8,64,128]{2,1,0:T(8,128)(2,1)S(1)}) custom-call(bf16[64,128]{1,0:T(8,128)(2,1)} %bitcast.8, bf16[128,512]{1,0:T(8,128)(2,1)} %bitcast.5, bf16[128,512]{1,0:T(8,128)(2,1)} %bitcast.6, bf16[128,512]{1,0:T(8,128)(2,1)} %bitcast.7), custom_call_target="tpu_custom_call" | custom-call | tf_op jit(solution)/shard_map/prepare/pallas_call | solution.py:157
  1.0 3.0 %collective-permute-start = (bf16[320,512]{1,0:T(8,128)(2,1)S(1)}, bf16[320,512]{1,0:T(8,128)(2,1)S(1)}, u32[]{:S(2)}, u32[]{:S(2)}) collective-permute-start(bf16[320,512]{1,0:T(8,128)(2,1)S(1)} %get-tuple-element.12.bundle_ref), channel_id=1, source_target_pairs={{0,16},{16,0},{1,17},{17,1},{2,18},{18,2},{3,19},{19,3},{4,20},{20... | collective-permute-start | bytes 983048 | tf_op jit(solution)/shard_map/ppermute | solution.py:166
  4.0 9.7 %all_to_all.15.blocks_ref = bf16[8,64,128]{2,1,0:T(8,128)(2,1)S(1)} all-to-all(bf16[8,64,128]{2,1,0:T(8,128)(2,1)S(1)} %get-tuple-element.14), channel_id=1, replica_groups={{10,2,0,4,14,6,8,12},{11,3,1,5,15,7,9,13},{26,18,16,20,30,22,24,28},{27..., dimensions={0} | all-to-all | bytes 262144 | tf_op jit(solution)/shard_map/all_to_all | solution.py:27
  13.8 0.0 collective-permute-done.other_ref
  13.8 0.3 shard_map.46
  14.0 8.8 %all_to_all.16.blocks_ref = bf16[8,64,128]{2,1,0:T(8,128)(2,1)S(1)} all-to-all(bf16[8,64,128]{2,1,0:T(8,128)(2,1)S(1)} %get-tuple-element.18), channel_id=1, replica_groups={{10,2,0,4,14,6,8,12},{11,3,1,5,15,7,9,13},{26,18,16,20,30,22,24,28},{27..., dimensions={0} | all-to-all | bytes 262144 | tf_op jit(solution)/shard_map/all_to_all | solution.py:27
  22.9 0.3 shard_map.47
  23.1 8.8 %all_to_all.17.blocks_ref = bf16[8,64,128]{2,1,0:T(8,128)(2,1)S(1)} all-to-all(bf16[8,64,128]{2,1,0:T(8,128)(2,1)S(1)} %shard_map.47), channel_id=1, replica_groups={{10,2,0,4,14,6,8,12},{11,3,1,5,15,7,9,13},{26,18,16,20,30,22,24,28},{27..., dimensions={0} | all-to-all | bytes 262144 | tf_op jit(solution)/shard_map/all_to_all | solution.py:27
  31.9 0.9 %shard_map.48 = bf16[64,128]{1,0:T(8,128)(2,1)} custom-call(bf16[320,512]{1,0:T(8,128)(2,1)S(1)} %get-tuple-element.12.bundle_ref, bf16[128,512]{1,0:T(8,128)(2,1)S(1)} %get-tuple-element.13.upper_ref, f32[64,128]{1,0:T(8,128)S(1)} %get-tuple-element.17.scaled_ref, bf16[8,64,128]{2,1,0:T(8,128)(2,1)S(1)} %all_to_all.17.blocks_ref), custom_call_target="tpu_custom_call" | custom-call | tf_op jit(solution)/shard_map/pallas_call | solution.py:171
Async XLA Ops:
  1.0 12.7 %collective-permute-start = (bf16[320,512]{1,0:T(8,128)(2,1)S(1)}, bf16[320,512]{1,0:T(8,128)(2,1)S(1)}, u32[]{:S(2)}, u32[]{:S(2)}) collective-permute-start(bf16[320,512]{1,0:T(8,128)(2,1)S(1)} %get-tuple-element.12.bundle_ref), channel_id=1, source_target_pairs={{0,16},{16,0},{1,17},{17,1},{2,18},{18,2},{3,19},{19,3},{4,20},{20... | collective-permute-start | bytes 983048 | tf_op jit(solution)/shard_map/ppermute | solution.py:166

commit v8 on v4

--- a/solution.py
+++ b/solution.py
@@ -14,7 +14,7 @@
     return lax.ppermute(block, axis, route)
 
 
-MEASURED = {8: (5, 1, 0, 2, 7, 3, 4, 6)}
+MEASURED = {8: (5, 3, 0, 2, 7, 1, 4, 6)}
 
 
 def group_order(devices):
@@ -65,26 +65,30 @@
 
 def prepare_kernel(src_ref, forward_ref, inverse_ref, upper_ref, bundle_ref, upper_out_ref, copies_ref, sems):
     forward_part, inverse_part, src_part = bundled(bundle_ref, forward_ref.shape[0], src_ref.shape)
-    both = [(src_ref, src_part), (inverse_ref, inverse_part)]
-    first_only = [(upper_ref, upper_out_ref)] + [(src_ref, copies_ref.at[i]) for i in range(copies_ref.shape[0])]
-    second_only = [(forward_ref, forward_part)]
 
     def bring(pairs):
         moves = [pltpu.make_async_copy(a, b, sems.at[i]) for i, (a, b) in enumerate(pairs)]
         for move in moves:
             move.start()
-        for move in moves:
+        return moves
+
+    first = lax.axis_index("sect") == 0
+
+    @pl.when(first)
+    def _():
+        moves = bring([(src_ref, copies_ref.at[0]), (inverse_ref, inverse_part), (upper_ref, upper_out_ref)])
+        moves[0].wait()
+        rows = copies_ref[0]
+        src_part[...] = rows
+        for i in range(1, copies_ref.shape[0]):
+            copies_ref[i] = rows
+        for move in moves[1:]:
             move.wait()
 
-    first = lax.axis_index("sect") == 0
-
-    @pl.when(first)
-    def _():
-        bring(first_only + both)
-
-    @pl.when(jnp.logical_not(first))
-    def _():
-        bring(second_only + both)
+    @pl.when(jnp.logical_not(first))
+    def _():
+        for move in bring([(forward_ref, forward_part), (inverse_ref, inverse_part), (src_ref, src_part)]):
+            move.wait()
 
 
 def forward_kernel(height, other_ref, blocks_ref, copies_ref):
@@ -143,7 +147,7 @@
         in_specs=[pl.BlockSpec(memory_space=pltpu.HBM)] * 4,
         out_specs=[vmem] * 3,
         out_shape=[bundle_shape, jax.ShapeDtypeStruct(upper.shape, upper.dtype), copies_shape],
-        scratch_shapes=[pltpu.SemaphoreType.DMA((devices + 3,))],
+        scratch_shapes=[pltpu.SemaphoreType.DMA((3,))],
         compiler_params=small,
         name="prepare",
     )(*(pltpu.with_memory_space_constraint(array, pltpu.HBM) for array in (src, forward, inverse, upper)))

time: 33.1 us -> 33.1 us (level)
  no operation moved by 1% of the time
where the time goes in v8:
time: 33.1 us; the launch traced here: 32.8 us
  blocking collectives  27.3 us (82%)
  starting transfers between devices  3.02 us (9%)
  Pallas kernels  2.4 us (7%)
    all_to_all x3, blocking collectives, exchange(): lax.all_to_all(copies, 'slab', split_axis=0, concat_axis=0, axis_index_gr...  27.3 us
    ppermute x1, starting transfers between devices, two_sections(): other = lax.ppermute(bundle, 'sect', [(0, 1), (1, 0)])  3.02 us
    pallas_call x3, Pallas kernels, local(): pl.pallas_call(functools.partial(kernel, height), in_specs=[vmem] * len(o...  1.4 us
    pallas_call x1, Pallas kernels, two_sections(): pl.pallas_call(prepare_kernel, in_specs=[pl.BlockSpec(memory_space=pltpu....  1.01 us
  transfers between devices with their start and end apart: 1, of which 0 were waited for; matrix products, arithmetic and copies ran while one was open for 0% of the time, Pallas kernels for 0%

profile of v8, /device:TPU:0, one launch (start us, length us, event | category | flops | bytes accessed | tf_op | source)
XLA Modules:
  0.0 32.8 jit_solution(9100187245199310834)
XLA Ops:
  0.0 1.0 %prepare.1 = (bf16[320,512]{1,0:T(8,128)(2,1)S(1)}, bf16[128,512]{1,0:T(8,128)(2,1)S(1)}, bf16[8,64,128]{2,1,0:T(8,128)(2,1)S(1)}) custom-call(bf16[64,128]{1,0:T(8,128)(2,1)} %bitcast.8, bf16[128,512]{1,0:T(8,128)(2,1)} %bitcast.5, bf16[128,512]{1,0:T(8,128)(2,1)} %bitcast.6, bf16[128,512]{1,0:T(8,128)(2,1)} %bitcast.7), custom_call_target="tpu_custom_call" | custom-call | tf_op jit(solution)/shard_map/prepare/pallas_call | solution.py:145
  1.0 3.0 %collective-permute-start = (bf16[320,512]{1,0:T(8,128)(2,1)S(1)}, bf16[320,512]{1,0:T(8,128)(2,1)S(1)}, u32[]{:S(2)}, u32[]{:S(2)}) collective-permute-start(bf16[320,512]{1,0:T(8,128)(2,1)S(1)} %get-tuple-element.10.bundle_ref), channel_id=1, source_target_pairs={{0,16},{16,0},{1,17},{17,1},{2,18},{18,2},{3,19},{19,3},{4,20},{20... | collective-permute-start | bytes 983048 | tf_op jit(solution)/shard_map/ppermute | solution.py:154
  4.0 9.7 %all_to_all.15.blocks_ref.src_blocks_ref = bf16[8,64,128]{2,1,0:T(8,128)(2,1)S(1)} all-to-all(bf16[8,64,128]{2,1,0:T(8,128)(2,1)S(1)} %get-tuple-element.12), channel_id=1, replica_groups={{10,6,0,4,14,2,8,12},{11,7,1,5,15,3,9,13},{26,22,16,20,30,18,24,28},{27..., dimensions={0} | all-to-all | bytes 262144 | tf_op jit(solution)/shard_map/all_to_all | solution.py:27
  13.8 0.0 collective-permute-done.other_ref
  13.8 0.2 shard_map.46
  14.0 8.8 %all_to_all.16.blocks_ref = bf16[8,64,128]{2,1,0:T(8,128)(2,1)S(1)} all-to-all(bf16[8,64,128]{2,1,0:T(8,128)(2,1)S(1)} %shard_map.46), channel_id=1, replica_groups={{10,6,0,4,14,2,8,12},{11,7,1,5,15,3,9,13},{26,22,16,20,30,18,24,28},{27..., dimensions={0} | all-to-all | bytes 262144 | tf_op jit(solution)/shard_map/all_to_all | solution.py:27
  22.8 0.3 shard_map.47
  23.1 8.8 %all_to_all.17.blocks_ref = bf16[8,64,128]{2,1,0:T(8,128)(2,1)S(1)} all-to-all(bf16[8,64,128]{2,1,0:T(8,128)(2,1)S(1)} %shard_map.47), channel_id=1, replica_groups={{10,6,0,4,14,2,8,12},{11,7,1,5,15,3,9,13},{26,22,16,20,30,18,24,28},{27..., dimensions={0} | all-to-all | bytes 262144 | tf_op jit(solution)/shard_map/all_to_all | solution.py:27
  31.9 0.9 %shard_map.48 = bf16[64,128]{1,0:T(8,128)(2,1)} custom-call(bf16[320,512]{1,0:T(8,128)(2,1)S(1)} %get-tuple-element.10.bundle_ref, bf16[128,512]{1,0:T(8,128)(2,1)S(1)} %get-tuple-element.11.upper_ref, bf16[8,64,128]{2,1,0:T(8,128)(2,1)S(1)} %all_to_all.15.blocks_ref.src_blocks_ref, bf16[8,64,128]{2,1,0:T(8,128)(2,1)S(1)} %all_to_all.17.blocks_ref), custom_call_target="tpu_custom_call" | custom-call | tf_op jit(solution)/shard_map/pallas_call | solution.py:159
Async XLA Ops:
  1.0 12.8 %collective-permute-start = (bf16[320,512]{1,0:T(8,128)(2,1)S(1)}, bf16[320,512]{1,0:T(8,128)(2,1)S(1)}, u32[]{:S(2)}, u32[]{:S(2)}) collective-permute-start(bf16[320,512]{1,0:T(8,128)(2,1)S(1)} %get-tuple-element.10.bundle_ref), channel_id=1, source_target_pairs={{0,16},{16,0},{1,17},{17,1},{2,18},{18,2},{3,19},{19,3},{4,20},{20... | collective-permute-start | bytes 983048 | tf_op jit(solution)/shard_map/ppermute | solution.py:154
